TPU v7x, 256 devices: a whole 4x4x8 slice. The times are simulated.
256 devices in a mesh: dp: 2 (over x_lo), context: 8 (over z), tensor: 16 (over y, x_hi, core).
Axes of the slice: x: 4 (x_hi: 2, x_lo: 2; x = x_hi * 2 + x_lo), y: 4, z: 8, core: 2. Of those that a mesh axis runs over, the one named last changes fastest.
Arguments:
- activations: bfloat16 [2, 4096, 4096], P('dp', ('context', 'tensor')), may hold values from -60 to 60
- in_weight: bfloat16 [4096, 3, 4096], P('dp', None, 'tensor'), may hold values from -0.09375 to 0.09375
- out_weight: bfloat16 [4096, 4096], P('tensor', 'dp'), may hold values from -0.09375 to 0.09375
- short_filter: float32 [3, 3, 4096], P(None, None, 'tensor'), may hold values from -2 to 2
- mixer_filter: float32 [128, 256], P(None, 'tensor'), may hold values from -0.5 to 0.5
- cotangent: bfloat16 [2, 4096, 4096], P('dp', ('context', 'tensor')), may hold values from -6 to 6
Outputs:
- block_out: bfloat16 [2, 4096, 4096], P('dp', ('context', 'tensor'))
- grad_input: bfloat16 [2, 4096, 4096], P('dp', ('context', 'tensor'))
- grad_in_weight: bfloat16 [4096, 3, 4096], P(('dp', 'context'), None, 'tensor')
- grad_out_weight: bfloat16 [4096, 4096], P('tensor', ('dp', 'context'))
- grad_short: float32 [3, 3, 4096], P(None, None, 'tensor')
- grad_mixer: float32 [128, 256], P(None, 'tensor')
All inputs are finite; a program needn't handle non-finite values.
Results may differ from a plain program's by a relative error of at most 0.019.
Values may be sent and summed in bfloat16 or wider, within the bound.
A program may use at most 128 MiB of HBM per device.

v0:
```python
import jax
import jax.numpy as jnp
from jax import lax
from jax.sharding import PartitionSpec as P

EPS = 1e-05


def from_behind(value, axis, steps):
    count = lax.axis_size(axis)
    initial, last = (max(0, -steps), min(count, count - steps))
    return lax.ppermute(value, axis, [(source, source + steps) for source in range(initial, last)])


def skew_table(base, span):
    groups = base.shape[0]
    padded = jnp.concatenate([base, jnp.zeros((groups, span + 1), jnp.float32)], axis=1)
    tiled = jnp.tile(padded[:, None, :], (1, span, 1)).reshape(groups, span * (2 * span + 1))
    return tiled[:, : span * 2 * span].reshape(groups, span, 2 * span)


def band_windows(extended, span, groups):
    chans = extended.shape[1]
    padded = jnp.concatenate([extended, jnp.zeros((1, chans), jnp.float32)], 0)
    blocks = padded.shape[0] // span
    padded = padded.reshape(blocks, span, groups, chans // groups)
    return jnp.concatenate([padded[:-1], padded[1:]], axis=1)


def band_apply(table, extended, span):
    groups = table.shape[0]
    chans = extended.shape[1]
    windows = band_windows(extended, span, groups)
    result = jnp.einsum("gtu,bugc->btgc", table, windows, precision=lax.Precision.HIGHEST)
    return result.reshape(windows.shape[0] * span, chans)


def band_grad(left, extended, span, groups):
    rows, chans = left.shape
    lhs = left.reshape(rows // span, span, groups, chans // groups)
    windows = band_windows(extended, span, groups)
    prods = jnp.einsum("btgc,bugc->gtu", lhs, windows, precision=lax.Precision.HIGHEST)
    flat = jnp.concatenate(
        [prods.reshape(groups, span * 2 * span), jnp.zeros((groups, span), jnp.float32)], axis=1
    )
    skewed = flat.reshape(groups, span, 2 * span + 1).sum(axis=1)
    return jnp.flip(skewed[:, :span], axis=1).T


def short_apply(filters, extended, rows):
    taps = filters.shape[1]
    total = jnp.zeros((rows,) + extended.shape[1:], jnp.float32)
    for tap in range(taps):
        total = total + filters[:, tap][None] * extended[taps - 1 - tap : taps - 1 - tap + rows]
    return total


def per_device(activations, in_weight, out_weight, short_filter, mixer_filter, cotangent):
    rows_own = activations.shape[1]
    width = activations.shape[2]
    rows = rows_own * lax.axis_size("tensor")
    span = mixer_filter.shape[0]
    groups = mixer_filter.shape[1]
    taps = short_filter.shape[1]
    chans = short_filter.shape[2]
    own = activations[0].astype(jnp.float32)
    inverse = lax.rsqrt(jnp.mean(own * own, axis=-1, keepdims=True) + EPS)
    normed = (own * inverse).astype(jnp.bfloat16)
    slab = lax.all_gather(normed, "tensor", axis=0, tiled=True)
    full_in, full_out = (
        lax.all_gather(in_weight, "dp", axis=0, tiled=True),
        lax.all_gather(out_weight, "dp", axis=1, tiled=True),
    )
    in_flat = full_in.reshape(width, 3 * chans)
    projected = (
        jnp.dot(slab, in_flat, preferred_element_type=jnp.float32)
        .astype(jnp.bfloat16)
        .reshape(rows, 3, chans)
    )
    proj_wide = projected.astype(jnp.float32)
    table_fwd = skew_table(jnp.flip(mixer_filter, axis=0).T, span)
    table_back = skew_table(mixer_filter.T, span)
    short_rim = from_behind(projected[rows - taps + 1 :], "context", 1)
    proj_ext = jnp.concatenate([short_rim.astype(jnp.float32), proj_wide], 0)
    streams = short_apply(short_filter, proj_ext, rows)
    gated = (streams[:, 1] * streams[:, 2]).astype(jnp.bfloat16)
    gate_rim = from_behind(gated[rows - span + 1 :], "context", 1)
    gate_ext = jnp.concatenate([gate_rim, gated], 0).astype(jnp.float32)
    mixed = band_apply(table_fwd, gate_ext, span)
    output_rows = (streams[:, 0] * mixed).astype(jnp.bfloat16)
    piece = output_rows
    branch = lax.psum_scatter(
        jnp.dot(piece, full_out, preferred_element_type=jnp.float32).astype(jnp.bfloat16),
        "tensor",
        scatter_dimension=0,
        tiled=True,
    ).astype(jnp.float32)
    block_out = (own + branch).astype(jnp.bfloat16)[None]
    cot_slab = lax.all_gather(cotangent[0], "tensor", axis=0, tiled=True)
    grad_rows = lax.dot_general(
        cot_slab, full_out, (((1,), (1,)), ((), ())), preferred_element_type=jnp.float32
    )
    out_term = lax.dot_general(
        output_rows, cot_slab, (((0,), (0,)), ((), ())), preferred_element_type=jnp.float32
    )
    grad_mix = (grad_rows * streams[:, 0]).astype(jnp.bfloat16)
    grad_mix_wide = grad_mix.astype(jnp.float32)
    mix_rim = from_behind(grad_mix[: span - 1], "context", -1)
    grad_gate = band_apply(
        table_back, jnp.concatenate([grad_mix_wide, mix_rim.astype(jnp.float32)], 0), span
    )
    mixer_term = band_grad(grad_mix_wide, gate_ext, span, groups)
    grad_streams = jnp.stack(
        [grad_rows * mixed, grad_gate * streams[:, 2], grad_gate * streams[:, 1]], axis=1
    )
    stream_rim = from_behind(grad_streams[: taps - 1], "context", -1)
    stream_ext = jnp.concatenate([grad_streams, stream_rim], 0)
    grad_proj = jnp.zeros((rows, 3, chans), jnp.float32)
    for tap in range(taps):
        grad_proj = grad_proj + short_filter[:, tap][None] * stream_ext[tap : tap + rows]
    grad_proj = grad_proj.astype(jnp.bfloat16)
    short_terms = [
        jnp.sum(grad_streams * proj_ext[taps - 1 - tap : taps - 1 - tap + rows], axis=0)
        for tap in range(taps)
    ]
    short_term = jnp.stack(short_terms, axis=1)
    grad_short, grad_mixer = lax.psum((short_term, mixer_term), ("dp", "context"))
    proj_flat = grad_proj.reshape(rows, 3 * chans)
    in_term = lax.dot_general(
        slab, proj_flat, (((0,), (0,)), ((), ())), preferred_element_type=jnp.float32
    ).reshape(width, 3, chans)
    grad_in, grad_out = (
        lax.psum_scatter(
            in_term.astype(jnp.bfloat16), ("dp", "context"), scatter_dimension=0, tiled=True
        ).astype(jnp.float32),
        lax.psum_scatter(
            out_term.astype(jnp.bfloat16), ("dp", "context"), scatter_dimension=1, tiled=True
        ).astype(jnp.float32),
    )
    piece = proj_flat
    grad_norm = lax.psum_scatter(
        lax.dot_general(
            piece, in_flat, (((1,), (1,)), ((), ())), preferred_element_type=jnp.float32
        ).astype(jnp.bfloat16),
        "tensor",
        scatter_dimension=0,
        tiled=True,
    ).astype(jnp.float32)
    grad_x = (
        cotangent[0].astype(jnp.float32)
        + inverse * grad_norm
        - own * inverse**3 * jnp.mean(grad_norm * own, axis=-1, keepdims=True)
    )
    grad_input = grad_x.astype(jnp.bfloat16)[None]
    return (
        block_out,
        grad_input,
        grad_in.astype(jnp.bfloat16),
        grad_out.astype(jnp.bfloat16),
        grad_short,
        grad_mixer,
    )


def solution(mesh):
    placed = (
        P("dp", ("context", "tensor"), None),
        P("dp", None, "tensor"),
        P("tensor", "dp"),
        P(None, None, "tensor"),
        P(None, "tensor"),
        P("dp", ("context", "tensor"), None),
    )
    return jax.shard_map(
        per_device,
        mesh=mesh,
        in_specs=placed,
        out_specs=(
            P("dp", ("context", "tensor"), None),
            P("dp", ("context", "tensor"), None),
            P(("dp", "context"), None, "tensor"),
            P("tensor", ("dp", "context")),
            P(None, None, "tensor"),
            P(None, "tensor"),
        ),
        check_vma=False,
    )
```

profile of v0, /device:TPU:2, one launch (start us, length us, event | category | flops | bytes accessed | tf_op | source)
XLA Modules:
  0.0 681.2 jit_solution(12522044125238099399)
XLA Ops:
  10.5 86.5 %all-gather.8.cloned.1.call-done = bf16[4096,3,256]{2,0,1:T(8,128)(2,1)} async-done(((bf16[2048,3,256]{2,0,1:T(8,128)(2,1)}), bf16[4096,3,256]{2,0,1:T(8,128)(2,1)}) %all-gather.8.cloned.1.call-update) | async-done | bytes 6291472 | tf_op jit(solution)/shard_map/all_gather | solution.py:71
  97.1 8.7 %copy.20 = bf16[4096,3,256]{0,2,1:T(8,128)(2,1)} copy(bf16[4096,3,256]{2,0,1:T(8,128)(2,1)} %all-gather.8.cloned.1.call-done) | data formatting | bytes 12582912 | tf_op jit(solution)/shard_map/all_gather | solution.py:71
  105.8 55.7 %all-gather.6.cloned.1.call-done = bf16[512,4096]{1,0:T(8,128)(2,1)} async-done(((bf16[32,4096]{1,0:T(8,128)(2,1)}), bf16[512,4096]{1,0:T(8,128)(2,1)}) %all-gather.6.cloned.1.call-update) | async-done | bytes 4194320 | tf_op jit(solution)/shard_map/all_gather | solution.py:69
  161.5 7.5 %convolution_convert_fusion.3 = bf16[512,768]{1,0:T(8,128)(2,1)S(1)} fusion(bf16[512,4096]{1,0:T(8,128)(2,1)} %all-gather.6.cloned.1.call-done, bf16[4096,768]{0,1:T(8,128)(2,1)} %bitcast.133), kind=kOutput, calls=%fused_computation.27 | convolution fusion | flops 3221618688 | bytes 11272192 | tf_op jit(solution)/shard_map/dot_general | solution.py:76
  169.1 3.5 collective-permute-start
  174.3 24.9 %all-gather.10.cloned.1.call-done = bf16[256,4096]{1,0:T(8,128)(2,1)} async-done(((bf16[256,2048]{1,0:T(8,128)(2,1)}), bf16[256,4096]{1,0:T(8,128)(2,1)}) %all-gather.10.cloned.1.call-update) | async-done | bytes 2097168 | tf_op jit(solution)/shard_map/all_gather | solution.py:72
  199.2 63.7 %all-gather.12.cloned.1.call-done = bf16[1,512,4096]{2,1,0:T(8,128)(2,1)} async-done(((bf16[1,32,4096]{2,1,0:T(8,128)(2,1)}), bf16[1,512,4096]{2,1,0:T(8,128)(2,1)}) %all-gather.12.cloned.1.call-update) | async-done | bytes 4194320 | tf_op jit(solution)/shard_map/all_gather | solution.py:99
  262.9 5.2 fusion.36
  272.2 3.9 tile.17
  283.5 3.9 fusion.15
  290.1 4.7 collective-permute-start.1
  296.8 3.9 tile.15
  307.4 2.1 slice.105
  314.2 2.3 fusion.12
  321.1 4.2 collective-permute-done.3
  327.4 5.1 bitcast_convert_fusion
  334.0 3.3 convolution_convert_fusion.1
  337.4 4.8 convolution_convert_fusion.2
  343.7 8.6 %convolution_convert_fusion = bf16[4096,3,256]{2,0,1:T(8,128)(2,1)} fusion(bf16[512,4096]{1,0:T(8,128)(2,1)} %all-gather.6.cloned.1.call-done, bf16[512,3,256]{0,2,1:T(8,128)(2,1)S(1)} %copy.39), kind=kOutput, calls=%fused_computation.1 | convolution fusion | flops 3224371200 | bytes 11272192 | tf_op jit(solution)/shard_map/dot_general | solution.py:129
  359.2 3.7 reshape.99
  365.5 63.4 %all-reduce.4 = (f32[3,3,256]{2,0,1:T(4,128)S(1)}, f32[128,16]{0,1:T(8,128)}) all-reduce(f32[3,3,256]{2,0,1:T(4,128)S(1)} %pad_maximum_fusion.4, f32[128,16]{0,1:T(8,128)S(1)} %bitcast.141), channel_id=1, replica_groups=mesh['dp'=2,'context'=8,'tensor'=16] {'dp','context'}, use_global_device_ids=true, to_apply=%region_9.10 | all-reduce | flops 4352 | bytes 34816 | tf_op jit(solution)/shard_map/psum | solution.py:127
  430.6 80.0 %reduce-scatter.5.cloned.1.call-done = bf16[32,4096]{1,0:T(8,128)(2,1)} async-done(((bf16[512,4096]{1,0:T(8,128)(2,1)}), bf16[32,4096]{1,0:T(8,128)(2,1)}) %reduce-scatter.5.cloned.1.call-update) | async-done | bytes 262160 | tf_op jit(solution)/shard_map/reduce_scatter | solution.py:92
  512.7 75.1 %reduce-scatter.11.cloned.1.call-done = bf16[256,256]{1,0:T(8,128)(2,1)} async-done(((bf16[256,4096]{1,0:T(8,128)(2,1)}), bf16[256,256]{1,0:T(8,128)(2,1)}) %reduce-scatter.11.cloned.1.call-update) | async-done | bytes 131088 | tf_op jit(solution)/shard_map/reduce_scatter | solution.py:136
  587.7 86.6 %reduce-scatter.9.cloned.1.call-done = bf16[256,3,256]{2,0,1:T(8,128)(2,1)} async-done(((bf16[4096,3,256]{2,0,1:T(8,128)(2,1)}), bf16[256,3,256]{2,0,1:T(8,128)(2,1)}) %reduce-scatter.9.cloned.1.call-update) | async-done | bytes 393232 | tf_op jit(solution)/shard_map/reduce_scatter | solution.py:133
  (140 shorter events, 55.3 us)
Async XLA Ops:
  7.2 89.9 %all-gather.8.cloned.1.call-start = ((), (), s32[]{:S(2)}) async-start(), calls=%async_computation.5 | async-start | bytes 9437184 | tf_op jit(solution)/shard_map/all_gather | solution.py:71
  7.9 2.6 copy-start.20
  7.9 153.6 %all-gather.6.cloned.1.call-start = ((), (), s32[]{:S(2)}) async-start(), calls=%async_computation.4 | async-start | bytes 4456448 | tf_op jit(solution)/shard_map/all_gather | solution.py:69
  9.1 190.1 %all-gather.10.cloned.1.call-start = ((), (), s32[]{:S(2)}) async-start(), calls=%async_computation.6 | async-start | bytes 3145728 | tf_op jit(solution)/shard_map/all_gather | solution.py:72
  9.9 253.1 %all-gather.12.cloned.1.call-start = ((), (), s32[]{:S(2)}) async-start(), calls=%async_computation.11 | async-start | bytes 4456448 | tf_op jit(solution)/shard_map/all_gather | solution.py:99
  10.5 419.0 %reduce-scatter.7.cloned.1.call-start = ((), (), s32[]{:S(2)}) async-start(), calls=%async_computation.8 | async-start | bytes 4456448 | tf_op jit(solution)/shard_map/reduce_scatter | solution.py:141
  169.0 3.8 copy-start.7
  169.1 4.8 collective-permute-start
  174.3 93.9 %copy-start.5 = (f32[512,3,256]{2,0,1:T(8,128)}, f32[512,3,256]{2,0,1:T(8,128)S(1)}, u32[]{:S(2)}) copy-start(f32[512,3,256]{2,0,1:T(8,128)S(1)} %multiply_add_fusion) | copy-start | bytes 4718596
  174.3 95.9 %copy-start.19 = (f32[128,16]{0,1:T(8,128)S(1)}, f32[128,16]{0,1:T(8,128)}, u32[]{:S(2)}) copy-start(f32[128,16]{0,1:T(8,128)} %param.10) | copy-start | bytes 24580
  268.9 11.2 %collective-permute-start.2 = (bf16[127,256]{1,0:T(8,128)(2,1)S(1)}, bf16[127,256]{1,0:T(8,128)(2,1)S(1)}, u32[]{:S(2)}, u32[]{:S(2)}) collective-permute-start(bf16[127,256]{1,0:T(8,128)(2,1)S(1)} %slice.125), channel_id=1, source_target_pairs={{16,0},{32,16},{48,32},{64,48},{80,64},{96,80},{112,96},{17,1},{33... | collective-permute-start | bytes 195080 | tf_op jit(solution)/shard_map/ppermute | solution.py:12
  277.6 2.0 copy-start.14
  290.1 14.2 %collective-permute-start.1 = (bf16[127,256]{1,0:T(8,128)(2,1)S(1)}, bf16[127,256]{1,0:T(8,128)(2,1)S(1)}, u32[]{:S(2)}, u32[]{:S(2)}) collective-permute-start(bf16[127,256]{1,0:T(8,128)(2,1)S(1)} %slice_bitcast_fusion.1), channel_id=1, source_target_pairs={{0,16},{16,32},{32,48},{48,64},{64,80},{80,96},{96,112},{1,17},{17... | collective-permute-start | bytes 195080 | tf_op jit(solution)/shard_map/ppermute | solution.py:12
  302.3 2.0 copy-start.17
  310.4 3.3 copy-start.12
  313.8 2.7 copy-start.1
  317.8 9.6 %slice-start.2 = ((s8[6291456]{0:T(1024)(128)(4,1)}), s8[4194304]{0:T(1024)(128)(4,1)S(1)}, s32[]{:S(2)}) async-start(s8[6291456]{0:T(1024)(128)(4,1)} %bitcast.131), calls=%async_computation.14 | async-start | bytes 8388608
  319.6 7.8 %slice-start.3 = ((s8[6291456]{0:T(1024)(128)(4,1)}), s8[2097152]{0:T(1024)(128)(4,1)S(1)}, s32[]{:S(2)}) async-start(s8[6291456]{0:T(1024)(128)(4,1)} %bitcast.131), calls=%async_computation.15 | async-start | bytes 4194304
  319.6 5.8 collective-permute-start.3
  332.5 178.2 %reduce-scatter.5.cloned.1.call-start = ((), (), s32[]{:S(2)}) async-start(), calls=%async_computation.7 | async-start | bytes 4456448 | tf_op jit(solution)/shard_map/reduce_scatter | solution.py:92
  337.3 250.4 %reduce-scatter.11.cloned.1.call-start = ((), (), s32[]{:S(2)}) async-start(), calls=%async_computation.10 | async-start | bytes 2228224 | tf_op jit(solution)/shard_map/reduce_scatter | solution.py:136
  342.3 332.1 %reduce-scatter.9.cloned.1.call-start = ((), (), s32[]{:S(2)}) async-start(), calls=%async_computation.9 | async-start | bytes 6684672 | tf_op jit(solution)/shard_map/reduce_scatter | solution.py:133
  363.2 2.0 copy-start.8
  365.2 145.4 %copy-start.18 = (bf16[1,32,4096]{2,1,0:T(8,128)(2,1)S(1)}, bf16[1,32,4096]{2,1,0:T(8,128)(2,1)}, u32[]{:S(2)}) copy-start(bf16[1,32,4096]{2,1,0:T(8,128)(2,1)} %param.11) | copy-start | bytes 786436
  (13 other events, 16.8 us)
Sparse Core Ops, SparseCore 0:
  9.8 87.2 all-gather.7
  100.4 61.0 all-gather.5
  163.3 35.8 all-gather.9
  201.8 61.0 all-gather.11
  332.6 86.5 reduce-scatter.6
  423.3 87.2 reduce-scatter.4
  513.7 73.9 reduce-scatter.10
  590.9 83.4 reduce-scatter.8
where the time goes:
time: 683 us; the launch traced here: 681 us
  waiting for transfers between devices  479 us (70%)
  blocking collectives  63.4 us (9%)
  local copies, waits for them, and re-layouts  60.3 us (9%)
  matrix products  41.7 us (6%)
  between operations  14.6 us (2%)
  starting transfers between devices  11.6 us (2%)
  other arithmetic  10.4 us (2%)
    reduce_scatter x1, waiting for transfers between devices, per_device(): lax.psum_scatter(in_term.astype(jnp.bfloat16), ('dp', 'context'), scatter...  86.6 us
    all_gather x1, waiting for transfers between devices, per_device(): lax.all_gather(in_weight, 'dp', axis=0, tiled=True)  86.5 us
    reduce_scatter x1, waiting for transfers between devices, per_device(): lax.psum_scatter(jnp.dot(piece, full_out, preferred_element_type=jnp.floa...  80 us
    reduce_scatter x1, waiting for transfers between devices, per_device(): lax.psum_scatter(out_term.astype(jnp.bfloat16), ('dp', 'context'), scatte...  75.1 us
    all_gather x1, waiting for transfers between devices, per_device(): cot_slab = lax.all_gather(cotangent[0], 'tensor', axis=0, tiled=True)  63.7 us
    psum x1, blocking collectives, per_device(): lax.psum((short_term, mixer_term), ('dp', 'context'))  63.4 us
    all_gather x1, waiting for transfers between devices, per_device(): slab = lax.all_gather(normed, 'tensor', axis=0, tiled=True)  55.7 us
    all_gather x1, waiting for transfers between devices, per_device(): lax.all_gather(out_weight, 'dp', axis=1, tiled=True)  24.9 us
  transfers between devices with their start and end apart: 12, of which 9 were waited for; matrix products, arithmetic and copies ran while one was open for 10% of the time, Pallas kernels for 0%

commit v1 on v0

--- a/solution.py
+++ b/solution.py
@@ -10,6 +10,31 @@
     count = lax.axis_size(axis)
     initial, last = (max(0, -steps), min(count, count - steps))
     return lax.ppermute(value, axis, [(source, source + steps) for source in range(initial, last)])
+
+
+def pair_gather(value, axis, dim):
+    count = lax.axis_size(axis)
+    index = lax.axis_index(axis)
+    parts = [value]
+    for step in range(1, count):
+        parts.append(lax.ppermute(value, axis, [(i, (i + step) % count) for i in range(count)]))
+    shape = list(value.shape)
+    size = shape[dim]
+    shape[dim] = size * count
+    full = jnp.zeros(shape, value.dtype)
+    for step, part in enumerate(parts):
+        start = [0] * len(shape)
+        start[dim] = ((index - step) % count) * size
+        full = lax.dynamic_update_slice(full, part, start)
+    return full
+
+
+def scatter_sum(value, axis, dim):
+    count = lax.axis_size(axis)
+    shape = value.shape
+    split = shape[:dim] + (count, shape[dim] // count) + shape[dim + 1 :]
+    pieces = lax.all_to_all(value.reshape(split), axis, dim, 0)
+    return jnp.sum(pieces.astype(jnp.float32), axis=0)
 
 
 def skew_table(base, span):
@@ -67,10 +92,8 @@
     inverse = lax.rsqrt(jnp.mean(own * own, axis=-1, keepdims=True) + EPS)
     normed = (own * inverse).astype(jnp.bfloat16)
     slab = lax.all_gather(normed, "tensor", axis=0, tiled=True)
-    full_in, full_out = (
-        lax.all_gather(in_weight, "dp", axis=0, tiled=True),
-        lax.all_gather(out_weight, "dp", axis=1, tiled=True),
-    )
+    full_in = pair_gather(in_weight, "dp", 0)
+    full_out = pair_gather(out_weight, "dp", 1)
     in_flat = full_in.reshape(width, 3 * chans)
     projected = (
         jnp.dot(slab, in_flat, preferred_element_type=jnp.float32)
@@ -89,12 +112,11 @@
     mixed = band_apply(table_fwd, gate_ext, span)
     output_rows = (streams[:, 0] * mixed).astype(jnp.bfloat16)
     piece = output_rows
-    branch = lax.psum_scatter(
+    branch = scatter_sum(
         jnp.dot(piece, full_out, preferred_element_type=jnp.float32).astype(jnp.bfloat16),
         "tensor",
-        scatter_dimension=0,
-        tiled=True,
-    ).astype(jnp.float32)
+        0,
+    )
     block_out = (own + branch).astype(jnp.bfloat16)[None]
     cot_slab = lax.all_gather(cotangent[0], "tensor", axis=0, tiled=True)
     grad_rows = lax.dot_general(
@@ -138,14 +160,13 @@
         ).astype(jnp.float32),
     )
     piece = proj_flat
-    grad_norm = lax.psum_scatter(
+    grad_norm = scatter_sum(
         lax.dot_general(
             piece, in_flat, (((1,), (1,)), ((), ())), preferred_element_type=jnp.float32
         ).astype(jnp.bfloat16),
         "tensor",
-        scatter_dimension=0,
-        tiled=True,
-    ).astype(jnp.float32)
+        0,
+    )
     grad_x = (
         cotangent[0].astype(jnp.float32)
         + inverse * grad_norm

time: 683 us -> 472 us (0.69)
  waiting for transfers between devices: 479 us -> 230 us
  other arithmetic: 10.4 us -> 26.6 us
  starting transfers between devices: 11.6 us -> 24.5 us
  local copies, waits for them, and re-layouts: 60.3 us -> 71.6 us
    all_to_all x0 -> x2, waiting for transfers between devices: none -> 117 us  [scatter_sum(): pieces = lax.all_to_all(value.reshape(split), axis, dim, 0)]
    all_gather x2 -> x0, waiting for transfers between devices: 111 us -> none  [the longest x1 86.5 us: per_device(): lax.all_gather(in_weight, 'dp', axis=0, tiled=True)]
    reduce_scatter x1, waiting for transfers between devices: 86.6 us -> 0.01 us  [per_device(): lax.psum_scatter(in_term.astype(jnp.bfloat16), ('dp', 'context'), scatter...]
    ppermute x0 -> x2, waiting for transfers between devices: none -> 82.2 us  [pair_gather(): lax.ppermute(value, axis, [(i, (i + step) % count) for i in range(count)])]
    reduce_scatter x2 -> x0, waiting for transfers between devices: 80 us -> none  [the longest x1 80 us: per_device(): lax.psum_scatter(jnp.dot(piece, full_out, preferred_element_type=jnp.floa...]
    reduce_scatter x1, waiting for transfers between devices: 75.1 us -> 0.01 us  [per_device(): lax.psum_scatter(out_term.astype(jnp.bfloat16), ('dp', 'context'), scatte...]
    all_gather x1, waiting for transfers between devices: 55.7 us -> 0.01 us  [per_device(): slab = lax.all_gather(normed, 'tensor', axis=0, tiled=True)]
    all_gather x1, waiting for transfers between devices: 63.7 us -> 17 us  [per_device(): cot_slab = lax.all_gather(cotangent[0], 'tensor', axis=0, tiled=True)]
  transfers between devices with their start and end apart: 12 -> 12, of which waited for: 9 -> 5; matrix products, arithmetic and copies ran while one was open for 10% -> 20% of each run, Pallas kernels for 0% -> 0%
where the time goes in v1:
time: 472 us; the launch traced here: 470 us
  waiting for transfers between devices  230 us (49%)
  local copies, waits for them, and re-layouts  71.6 us (15%)
  blocking collectives  63.4 us (13%)
  matrix products  40.4 us (9%)
  other arithmetic  26.6 us (6%)
  starting transfers between devices  24.5 us (5%)
  between operations  14.2 us (3%)
    all_to_all x2, waiting for transfers between devices, scatter_sum(): pieces = lax.all_to_all(value.reshape(split), axis, dim, 0)  117 us
    ppermute x2, waiting for transfers between devices, pair_gather(): lax.ppermute(value, axis, [(i, (i + step) % count) for i in range(count)])  82.2 us
    psum x1, blocking collectives, per_device(): lax.psum((short_term, mixer_term), ('dp', 'context'))  63.4 us
    all_gather x1, waiting for transfers between devices, per_device(): cot_slab = lax.all_gather(cotangent[0], 'tensor', axis=0, tiled=True)  17 us
    unnamed x60, local copies, waits for them, and re-layouts  16.3 us
    ppermute x4, waiting for transfers between devices, from_behind(): lax.ppermute(value, axis, [(source, source + steps) for source in range(i...  13.1 us
    ppermute x4, starting transfers between devices, from_behind(): lax.ppermute(value, axis, [(source, source + steps) for source in range(i...  12.7 us
    another operation x4, local copies, waits for them, and re-layouts, skew_table(): jnp.tile(padded[:, None, :], (1, span, 1))  11.5 us
  transfers between devices with their start and end apart: 12, of which 5 were waited for; matrix products, arithmetic and copies ran while one was open for 20% of the time, Pallas kernels for 0%

profile of v1, /device:TPU:2, one launch (start us, length us, event | category | flops | bytes accessed | tf_op | source)
XLA Modules:
  0.0 470.3 jit_solution(5357234230657179776)
XLA Ops:
  11.9 4.7 %copy.21 = bf16[2048,3,256]{0,2,1:T(8,128)(2,1)} copy(bf16[2048,3,256]{2,0,1:T(8,128)(2,1)} %param.7) | data formatting | bytes 6291456 | tf_op args[1]
  24.0 3.9 constant_dynamic-update-slice_fusion.3
  27.9 74.3 %collective-permute-done = bf16[2048,3,256]{0,2,1:T(8,128)(2,1)} collective-permute-done((bf16[2048,3,256]{0,2,1:T(8,128)(2,1)}, bf16[2048,3,256]{0,2,1:T(8,128)(2,1)}, u32[]{:S(2)}, u32[]{:S(2)}) %collective-permute-start) | collective-permute-done | bytes 3145760 | tf_op jit(solution)/shard_map/ppermute | solution.py:20
  102.2 4.1 constant_dynamic-update-slice_fusion.2
  106.4 7.5 %convolution_convert_fusion.3 = bf16[512,768]{1,0:T(8,128)(2,1)S(1)} fusion(bf16[512,4096]{1,0:T(8,128)(2,1)} %all-gather.4.cloned.1.call-done, bf16[4096,768]{0,1:T(8,128)(2,1)} %bitcast.1), kind=kOutput, calls=%fused_computation.29 | convolution fusion | flops 3221618688 | bytes 11272192 | tf_op jit(solution)/shard_map/dot_general | solution.py:99
  114.1 4.3 collective-permute-start.1
  118.4 7.8 %collective-permute-done.3 = bf16[256,2048]{1,0:T(8,128)(2,1)} collective-permute-done((bf16[256,2048]{1,0:T(8,128)(2,1)}, bf16[256,2048]{1,0:T(8,128)(2,1)}, u32[]{:S(2)}, u32[]{:S(2)}) %collective-permute-start.3) | collective-permute-done | bytes 1048608 | tf_op jit(solution)/shard_map/ppermute | solution.py:20
  130.0 4.2 multiply_add_fusion
  134.3 17.0 %all-gather.6.cloned.1.call-done = bf16[1,512,4096]{2,1,0:T(8,128)(2,1)} async-done(((bf16[1,32,4096]{2,1,0:T(8,128)(2,1)}), bf16[1,512,4096]{2,1,0:T(8,128)(2,1)}) %all-gather.6.cloned.1.call-update) | async-done | bytes 4194320 | tf_op jit(solution)/shard_map/all_gather | solution.py:121
  151.3 4.5 fusion.42
  159.2 3.9 tile.17
  173.6 3.9 fusion.15
  181.7 5.2 %collective-permute-start.2 = (bf16[127,256]{0,1:T(8,128)(2,1)}, bf16[127,256]{0,1:T(8,128)(2,1)}, u32[]{:S(2)}, u32[]{:S(2)}) collective-permute-start(bf16[127,256]{0,1:T(8,128)(2,1)} %slice_bitcast_fusion.1), channel_id=1, source_target_pairs={{0,16},{16,32},{32,48},{48,64},{64,80},{80,96},{96,112},{1,17},{17... | collective-permute-start | bytes 195080 | tf_op jit(solution)/shard_map/ppermute | solution.py:12
  190.7 3.9 tile.15
  208.2 4.3 fusion.12
  221.3 13.0 %collective-permute-done.5 = f32[2,3,256]{0,2,1:T(8,128)S(1)} collective-permute-done((f32[2,3,256]{0,2,1:T(8,128)S(1)}, f32[2,3,256]{0,2,1:T(8,128)S(1)}, u32[]{:S(2)}, u32[]{:S(2)}) %collective-permute-start.5) | collective-permute-done | bytes 6176 | tf_op jit(solution)/shard_map/ppermute | solution.py:12
  234.6 3.4 multiply_reduce_fusion.1
  238.9 5.4 %convolution_convert_fusion = bf16[4096,3,256]{2,0,1:T(8,128)(2,1)} fusion(bf16[512,4096]{1,0:T(8,128)(2,1)S(1)} %copy-done.25, bf16[512,3,256]{0,2,1:T(8,128)(2,1)S(1)} %get-tuple-element.20), kind=kOutput, calls=%fused_computation.3 | convolution fusion | flops 3224371200 | bytes 11272192 | tf_op jit(solution)/shard_map/dot_general | solution.py:151
  248.5 4.7 all-to-all-start
  253.2 7.8 %bitcast_convert_fusion = bf16[512,4096]{1,0:T(8,128)(2,1)} fusion(bf16[512,3,256]{0,2,1:T(8,128)(2,1)S(1)} %copy-done.18, bf16[4096,3,256]{0,2,1:T(8,128)(2,1)} %constant_dynamic-update-slice_fusion.2), kind=kOutput, calls=%fused_computation | convolution fusion | flops 3223322624 | bytes 11272192 | tf_op jit(solution)/shard_map/dot_general | solution.py:164
  261.1 116.6 %all-to-all-done = bf16[16,32,4096]{2,1,0:T(8,128)(2,1)} async-done(((bf16[16,32,4096]{2,1,0:T(8,128)(2,1)}), bf16[16,32,4096]{2,1,0:T(8,128)(2,1)}, u32[]{:S(2)}, u32[]{:S(2)}) %all-to-all-start) | async-done | bytes 4194336 | tf_op jit(solution)/shard_map/all_to_all | solution.py:36
  377.7 4.7 all-to-all-start.1
  386.2 3.7 reshape.148
  392.5 63.4 %all-reduce.4 = (f32[3,3,256]{2,0,1:T(4,128)S(1)}, f32[128,16]{0,1:T(8,128)}) all-reduce(f32[3,3,256]{2,0,1:T(4,128)S(1)} %pad_maximum_fusion.4, f32[128,16]{0,1:T(8,128)S(1)} %bitcast.159), channel_id=1, replica_groups=mesh['dp'=2,'context'=8,'tensor'=16] {'dp','context'}, use_global_device_ids=true, to_apply=%region_9.10 | all-reduce | flops 4352 | bytes 34816 | tf_op jit(solution)/shard_map/psum | solution.py:149
  (139 shorter events, 79.6 us)
Async XLA Ops:
  7.2 99.2 %all-gather.4.cloned.1.call-start = ((), (), s32[]{:S(2)}) async-start(), calls=%async_computation.4 | async-start | bytes 4456448 | tf_op jit(solution)/shard_map/all_gather | solution.py:94
  11.1 140.2 %all-gather.6.cloned.1.call-start = ((), (), s32[]{:S(2)}) async-start(), calls=%async_computation.7 | async-start | bytes 4456448 | tf_op jit(solution)/shard_map/all_gather | solution.py:121
  11.9 7.1 %copy-start.21 = (f32[3,3,256]{2,1,0:T(4,128)S(1)}, f32[3,3,256]{2,1,0:T(4,128)}, u32[]{:S(2)}) copy-start(f32[3,3,256]{2,1,0:T(4,128)} %param.9) | copy-start | bytes 27652
  11.9 451.9 %reduce-scatter.5.cloned.1.call-start = ((), (), s32[]{:S(2)}) async-start(), calls=%async_computation.6 | async-start | bytes 2228224 | tf_op jit(solution)/shard_map/reduce_scatter | solution.py:158
  16.7 85.5 %collective-permute-start = (bf16[2048,3,256]{0,2,1:T(8,128)(2,1)}, bf16[2048,3,256]{0,2,1:T(8,128)(2,1)}, u32[]{:S(2)}, u32[]{:S(2)}) collective-permute-start(bf16[2048,3,256]{0,2,1:T(8,128)(2,1)} %copy.21), channel_id=1, source_target_pairs={{0,128},{128,0},{1,129},{129,1},{2,130},{130,2},{3,131},{131,3},{4... | collective-permute-start | bytes 9437192 | tf_op jit(solution)/shard_map/ppermute | solution.py:20
  18.9 107.2 %collective-permute-start.3 = (bf16[256,2048]{1,0:T(8,128)(2,1)}, bf16[256,2048]{1,0:T(8,128)(2,1)}, u32[]{:S(2)}, u32[]{:S(2)}) collective-permute-start(bf16[256,2048]{1,0:T(8,128)(2,1)} %param.8), channel_id=1, source_target_pairs={{0,128},{128,0},{1,129},{129,1},{2,130},{130,2},{3,131},{131,3},{4... | collective-permute-start | bytes 3145736 | tf_op jit(solution)/shard_map/ppermute | solution.py:20
  113.9 15.1 %copy-start.6 = (bf16[512,768]{1,0:T(8,128)(2,1)}, bf16[512,768]{1,0:T(8,128)(2,1)S(1)}, u32[]{:S(2)}) copy-start(bf16[512,768]{1,0:T(8,128)(2,1)S(1)} %convolution_convert_fusion.3) | copy-start | bytes 2359300
  114.1 14.9 %collective-permute-start.1 = (bf16[2,3,256]{0,2,1:T(8,128)(2,1)S(1)}, bf16[2,3,256]{0,2,1:T(8,128)(2,1)}, u32[]{:S(2)}, u32[]{:S(2)}) collective-permute-start(bf16[2,3,256]{0,2,1:T(8,128)(2,1)S(1)} %bitcast.156), channel_id=1, source_target_pairs={{0,16},{16,32},{32,48},{48,64},{64,80},{80,96},{96,112},{1,17},{17... | collective-permute-start | bytes 9224 | tf_op jit(solution)/shard_map/ppermute | solution.py:12
  134.2 23.1 %copy-start.19 = (f32[128,16]{0,1:T(8,128)S(1)}, f32[128,16]{0,1:T(8,128)}, u32[]{:S(2)}) copy-start(f32[128,16]{0,1:T(8,128)} %param.10) | copy-start | bytes 24580
  155.8 10.9 %copy-start.8 = (bf16[512,256]{0,1:T(8,128)(2,1)}, bf16[512,256]{0,1:T(8,128)(2,1)S(1)}, u32[]{:S(2)}) copy-start(bf16[512,256]{0,1:T(8,128)(2,1)S(1)} %get-tuple-element.17) | copy-start | bytes 786436
  155.8 13.7 %collective-permute-start.4 = (bf16[127,256]{0,1:T(8,128)(2,1)S(1)}, bf16[127,256]{0,1:T(8,128)(2,1)S(1)}, u32[]{:S(2)}, u32[]{:S(2)}) collective-permute-start(bf16[127,256]{0,1:T(8,128)(2,1)S(1)} %slice.125), channel_id=1, source_target_pairs={{16,0},{32,16},{48,32},{64,48},{80,64},{96,80},{112,96},{17,1},{33... | collective-permute-start | bytes 195080 | tf_op jit(solution)/shard_map/ppermute | solution.py:12
  181.7 16.6 %collective-permute-start.2 = (bf16[127,256]{0,1:T(8,128)(2,1)}, bf16[127,256]{0,1:T(8,128)(2,1)}, u32[]{:S(2)}, u32[]{:S(2)}) collective-permute-start(bf16[127,256]{0,1:T(8,128)(2,1)} %slice_bitcast_fusion.1), channel_id=1, source_target_pairs={{0,16},{16,32},{32,48},{48,64},{64,80},{80,96},{96,112},{1,17},{17... | collective-permute-start | bytes 195080 | tf_op jit(solution)/shard_map/ppermute | solution.py:12
  208.2 4.6 copy-start.11
  208.2 7.3 %copy-start.4 = (bf16[1,512,4096]{2,1,0:T(8,128)(2,1)S(1)}, bf16[1,512,4096]{2,1,0:T(8,128)(2,1)}, u32[]{:S(2)}) copy-start(bf16[1,512,4096]{2,1,0:T(8,128)(2,1)} %all-gather.6.cloned.1.call-done) | copy-start | bytes 12582916
  218.2 245.6 %reduce-scatter.3.cloned.1.call-start = ((), (), s32[]{:S(2)}) async-start(), calls=%async_computation.5 | async-start | bytes 6684672 | tf_op jit(solution)/shard_map/reduce_scatter | solution.py:155
  218.2 16.2 %copy-start.1 = (f32[512,1,256]{0,2,1:T(8,128)S(1)}, f32[512,1,256]{0,2,1:T(8,128)}, u32[]{:S(2)}) copy-start(f32[512,1,256]{0,2,1:T(8,128)} %get-tuple-element.24) | copy-start | bytes 1572868
  219.5 15.0 %copy-start = (f32[512,768]{0,1:T(8,128)S(1)}, f32[512,768]{0,1:T(8,128)}, u32[]{:S(2)}) copy-start(f32[512,768]{0,1:T(8,128)} %copy.23) | copy-start | bytes 4718596
  219.5 14.8 %collective-permute-start.5 = (f32[2,3,256]{0,2,1:T(8,128)S(1)}, f32[2,3,256]{0,2,1:T(8,128)S(1)}, u32[]{:S(2)}, u32[]{:S(2)}) collective-permute-start(f32[2,3,256]{0,2,1:T(8,128)S(1)} %slice.128), channel_id=1, source_target_pairs={{16,0},{32,16},{48,32},{64,48},{80,64},{96,80},{112,96},{17,1},{33... | collective-permute-start | bytes 18440 | tf_op jit(solution)/shard_map/ppermute | solution.py:12
  234.6 4.3 copy-start.25
  248.5 4.7 %copy-start.18 = (bf16[512,3,256]{0,2,1:T(8,128)(2,1)S(1)}, bf16[512,3,256]{0,2,1:T(8,128)(2,1)}, u32[]{:S(2)}) copy-start(bf16[512,3,256]{0,2,1:T(8,128)(2,1)} %copy-done.17) | copy-start | bytes 2359300
  248.5 129.1 %all-to-all-start = ((bf16[16,32,4096]{2,1,0:T(8,128)(2,1)}), bf16[16,32,4096]{2,1,0:T(8,128)(2,1)}, u32[]{:S(2)}, u32[]{:S(2)}) async-start(bf16[16,32,4096]{2,1,0:T(8,128)(2,1)} %bitcast.143), calls=%async_computation | async-start | bytes 8388608 | tf_op jit(solution)/shard_map/all_to_all | solution.py:36
  377.7 4.7 copy-start.9
  377.7 4.8 %copy-start.3 = (f32[4,256,16,16]{1,3,0,2:T(8,128)S(1)}, f32[4,256,16,16]{1,3,0,2:T(8,128)}, u32[]{:S(2)}) copy-start(f32[4,256,16,16]{1,3,0,2:T(8,128)} %copy_dynamic-update-slice_fusion) | copy-start | bytes 3145732
  377.7 81.8 %all-to-all-start.1 = ((bf16[16,32,4096]{2,1,0:T(8,128)(2,1)}), bf16[16,32,4096]{2,1,0:T(8,128)(2,1)}, u32[]{:S(2)}, u32[]{:S(2)}) async-start(bf16[16,32,4096]{2,1,0:T(8,128)(2,1)} %bitcast.153), calls=%async_computation.1 | async-start | bytes 8388608 | tf_op jit(solution)/shard_map/all_to_all | solution.py:36
  (16 other events, 31.1 us)
Sparse Core Ops, SparseCore 0:
  11.3 76.3 all-gather.3
  90.5 60.7 all-gather.5
  218.3 72.4 reduce-scatter.4
  293.8 83.9 reduce-scatter.2

commit v2 on v1

--- a/solution.py
+++ b/solution.py
@@ -29,6 +29,20 @@
     return full
 
 
+def tree_psum(value, axes):
+    for axis in axes:
+        count = lax.axis_size(axis)
+        if count & (count - 1):
+            value = lax.psum(value, axis)
+            continue
+        step = 1
+        while step < count:
+            partner = lax.ppermute(value, axis, [(i, i ^ step) for i in range(count)])
+            value = value + partner
+            step *= 2
+    return value
+
+
 def scatter_sum(value, axis, dim):
     count = lax.axis_size(axis)
     shape = value.shape
@@ -55,16 +69,22 @@
 def band_apply(table, extended, span):
     groups = table.shape[0]
     chans = extended.shape[1]
-    windows = band_windows(extended, span, groups)
-    result = jnp.einsum("gtu,bugc->btgc", table, windows, precision=lax.Precision.HIGHEST)
+    windows = band_windows(extended, span, groups).astype(jnp.bfloat16)
+    high = table.astype(jnp.bfloat16)
+    low = (table - high.astype(jnp.float32)).astype(jnp.bfloat16)
+    result = jnp.einsum(
+        "gtu,bugc->btgc", high, windows, preferred_element_type=jnp.float32
+    ) + jnp.einsum("gtu,bugc->btgc", low, windows, preferred_element_type=jnp.float32)
     return result.reshape(windows.shape[0] * span, chans)
 
 
 def band_grad(left, extended, span, groups):
     rows, chans = left.shape
     lhs = left.reshape(rows // span, span, groups, chans // groups)
-    windows = band_windows(extended, span, groups)
-    prods = jnp.einsum("btgc,bugc->gtu", lhs, windows, precision=lax.Precision.HIGHEST)
+    windows = band_windows(extended, span, groups).astype(jnp.bfloat16)
+    prods = jnp.einsum(
+        "btgc,bugc->gtu", lhs.astype(jnp.bfloat16), windows, preferred_element_type=jnp.float32
+    )
     flat = jnp.concatenate(
         [prods.reshape(groups, span * 2 * span), jnp.zeros((groups, span), jnp.float32)], axis=1
     )
@@ -146,7 +166,9 @@
         for tap in range(taps)
     ]
     short_term = jnp.stack(short_terms, axis=1)
-    grad_short, grad_mixer = lax.psum((short_term, mixer_term), ("dp", "context"))
+    flat = tree_psum(jnp.concatenate([short_term.ravel(), mixer_term.ravel()]), ("dp", "context"))
+    grad_short = flat[: short_term.size].reshape(short_term.shape)
+    grad_mixer = flat[short_term.size :].reshape(mixer_term.shape)
     proj_flat = grad_proj.reshape(rows, 3 * chans)
     in_term = lax.dot_general(
         slab, proj_flat, (((0,), (0,)), ((), ())), preferred_element_type=jnp.float32

time: 472 us -> 438 us (0.928)
  blocking collectives: 63.4 us -> 0 us
  waiting for transfers between devices: 230 us -> 269 us
  local copies, waits for them, and re-layouts: 71.6 us -> 62.7 us
    psum x1 -> x0, blocking collectives: 63.4 us -> none  [per_device(): lax.psum((short_term, mixer_term), ('dp', 'context'))]
    ppermute x0 -> x4, waiting for transfers between devices: none -> 53.1 us  [tree_psum(): partner = lax.ppermute(value, axis, [(i, i ^ step) for i in range(count)])]
    ppermute x2, waiting for transfers between devices: 82.2 us -> 62.2 us  [pair_gather(): lax.ppermute(value, axis, [(i, (i + step) % count) for i in range(count)])]
    all_gather x1, waiting for transfers between devices: 17 us -> 22.4 us  [per_device(): cot_slab = lax.all_gather(cotangent[0], 'tensor', axis=0, tiled=True)]
    slice x8 -> x6, local copies, waits for them, and re-layouts: 11.1 us -> 6.2 us  [band_windows(): return jnp.concatenate([padded[:-1], padded[1:]], axis=1)]
    unnamed x60 -> x68, local copies, waits for them, and re-layouts: 16.3 us -> 15.4 us
  transfers between devices with their start and end apart: 12 -> 16, of which waited for: 5 -> 11; matrix products, arithmetic and copies ran while one was open for 20% -> 20% of each run, Pallas kernels for 0% -> 0%
where the time goes in v2:
time: 438 us; the launch traced here: 436 us
  waiting for transfers between devices  269 us (61%)
  local copies, waits for them, and re-layouts  62.7 us (14%)
  matrix products  38.3 us (9%)
  other arithmetic  26.5 us (6%)
  starting transfers between devices  25.4 us (6%)
  between operations  14.4 us (3%)
    all_to_all x2, waiting for transfers between devices, scatter_sum(): pieces = lax.all_to_all(value.reshape(split), axis, dim, 0)  116 us
    ppermute x2, waiting for transfers between devices, pair_gather(): lax.ppermute(value, axis, [(i, (i + step) % count) for i in range(count)])  62.2 us
    ppermute x4, waiting for transfers between devices, tree_psum(): partner = lax.ppermute(value, axis, [(i, i ^ step) for i in range(count)])  53.1 us
    all_gather x1, waiting for transfers between devices, per_device(): cot_slab = lax.all_gather(cotangent[0], 'tensor', axis=0, tiled=True)  22.4 us
    unnamed x68, local copies, waits for them, and re-layouts  15.4 us
    ppermute x4, waiting for transfers between devices, from_behind(): lax.ppermute(value, axis, [(source, source + steps) for source in range(i...  14.5 us
    another operation x4, local copies, waits for them, and re-layouts, skew_table(): jnp.tile(padded[:, None, :], (1, span, 1))  11.5 us
    ppermute x4, starting transfers between devices, from_behind(): lax.ppermute(value, axis, [(source, source + steps) for source in range(i...  9.97 us
  transfers between devices with their start and end apart: 16, of which 11 were waited for; matrix products, arithmetic and copies ran while one was open for 20% of the time, Pallas kernels for 0%

profile of v2, /device:TPU:2, one launch (start us, length us, event | category | flops | bytes accessed | tf_op | source)
XLA Modules:
  0.0 436.3 jit_solution(13535280192753381745)
XLA Ops:
  19.7 3.9 tile.17
  28.9 3.9 tile.15
  46.7 53.9 %collective-permute-done = bf16[2048,3,256]{0,2,1:T(8,128)(2,1)} collective-permute-done((bf16[2048,3,256]{0,2,1:T(8,128)(2,1)S(1)}, bf16[2048,3,256]{0,2,1:T(8,128)(2,1)}, u32[]{:S(2)}, u32[]{:S(2)}) %collective-permute-start) | collective-permute-done | bytes 3145760 | tf_op jit(solution)/shard_map/ppermute | solution.py:20
  100.6 4.1 constant_dynamic-update-slice_fusion.4
  104.7 7.5 %convolution_convert_fusion.3 = bf16[512,768]{1,0:T(8,128)(2,1)S(1)} fusion(bf16[512,4096]{1,0:T(8,128)(2,1)} %all-gather.4.cloned.1.call-done, bf16[4096,768]{0,1:T(8,128)(2,1)} %bitcast.1), kind=kOutput, calls=%fused_computation.31 | convolution fusion | flops 3221618688 | bytes 11272192 | tf_op jit(solution)/shard_map/dot_general | solution.py:119
  112.4 3.8 collective-permute-start.1
  116.2 8.3 %collective-permute-done.3 = bf16[256,2048]{1,0:T(8,128)(2,1)} collective-permute-done((bf16[256,2048]{1,0:T(8,128)(2,1)}, bf16[256,2048]{1,0:T(8,128)(2,1)}, u32[]{:S(2)}, u32[]{:S(2)}) %collective-permute-start.3) | collective-permute-done | bytes 1048608 | tf_op jit(solution)/shard_map/ppermute | solution.py:20
  128.9 22.4 %all-gather.6.cloned.1.call-done = bf16[1,512,4096]{2,1,0:T(8,128)(2,1)} async-done(((bf16[1,32,4096]{2,1,0:T(8,128)(2,1)}), bf16[1,512,4096]{2,1,0:T(8,128)(2,1)}) %all-gather.6.cloned.1.call-update) | async-done | bytes 4194320 | tf_op jit(solution)/shard_map/all_gather | solution.py:141
  151.3 4.9 %multiply_convert_fusion = (bf16[512,256]{0,1:T(8,128)(2,1)S(1)}, f32[512,256]{0,1:T(8,128)}) fusion(f32[512,3,256]{0,2,1:T(8,128)S(1)} %multiply_add_fusion, bf16[256,4096]{1,0:T(8,128)(2,1)} %constant_dynamic-update-slice_fusion.2, bf16[1,512,4096]{2,1,0:T(8,128)(2,1)} %all-gather.6.cloned.1.call-done), kind=kOutput, calls=%fused_computation.64 | convolution fusion | flops 1074003968 | bytes 7602176 | tf_op jit(solution)/shard_map/dot_general | solution.py:142
  161.7 4.1 collective-permute-done.4
  175.4 3.5 collective-permute-start.2
  195.5 10.2 %collective-permute-done.5 = f32[2,3,256]{0,2,1:T(8,128)S(1)} collective-permute-done((f32[2,3,256]{0,2,1:T(8,128)S(1)}, f32[2,3,256]{0,2,1:T(8,128)S(1)}, u32[]{:S(2)}, u32[]{:S(2)}) %collective-permute-start.5) | collective-permute-done | bytes 6176 | tf_op jit(solution)/shard_map/ppermute | solution.py:12
  205.9 3.5 multiply_reduce_fusion.1
  210.3 5.4 %convolution_convert_fusion = bf16[4096,3,256]{2,0,1:T(8,128)(2,1)} fusion(bf16[512,4096]{1,0:T(8,128)(2,1)S(1)} %copy-done.27, bf16[512,3,256]{0,2,1:T(8,128)(2,1)S(1)} %get-tuple-element.26), kind=kOutput, calls=%fused_computation.3 | convolution fusion | flops 3224371200 | bytes 11272192 | tf_op jit(solution)/shard_map/dot_general | solution.py:173
  216.6 4.9 %convolution_convert_fusion.1 = bf16[512,4096]{1,0:T(8,128)(2,1)} fusion(bf16[512,256]{0,1:T(8,128)(2,1)S(1)} %copy-done.14, bf16[256,4096]{1,0:T(8,128)(2,1)} %constant_dynamic-update-slice_fusion.2), kind=kOutput, calls=%fused_computation.4 | convolution fusion | flops 1075838976 | bytes 6553600 | tf_op jit(solution)/shard_map/dot_general | solution.py:136
  221.5 4.9 %all-to-all-start = ((bf16[16,32,4096]{2,1,0:T(8,128)(2,1)}), bf16[16,32,4096]{2,1,0:T(8,128)(2,1)}, u32[]{:S(2)}, u32[]{:S(2)}) async-start(bf16[16,32,4096]{2,1,0:T(8,128)(2,1)} %bitcast.157), calls=%async_computation | async-start | bytes 8388608 | tf_op jit(solution)/shard_map/all_to_all | solution.py:50
  226.5 7.9 %bitcast_convert_fusion = bf16[512,4096]{1,0:T(8,128)(2,1)} fusion(bf16[512,3,256]{0,2,1:T(8,128)(2,1)S(1)} %copy-done.18, bf16[4096,3,256]{0,2,1:T(8,128)(2,1)} %constant_dynamic-update-slice_fusion.4), kind=kOutput, calls=%fused_computation | convolution fusion | flops 3223322624 | bytes 11272192 | tf_op jit(solution)/shard_map/dot_general | solution.py:186
  234.3 116.0 %all-to-all-done = bf16[16,32,4096]{2,1,0:T(8,128)(2,1)} async-done(((bf16[16,32,4096]{2,1,0:T(8,128)(2,1)}), bf16[16,32,4096]{2,1,0:T(8,128)(2,1)}, u32[]{:S(2)}, u32[]{:S(2)}) %all-to-all-start) | async-done | bytes 4194336 | tf_op jit(solution)/shard_map/all_to_all | solution.py:50
  350.3 4.7 %all-to-all-start.1 = ((bf16[16,32,4096]{2,1,0:T(8,128)(2,1)}), bf16[16,32,4096]{2,1,0:T(8,128)(2,1)}, u32[]{:S(2)}, u32[]{:S(2)}) async-start(bf16[16,32,4096]{2,1,0:T(8,128)(2,1)} %bitcast.165), calls=%async_computation.1 | async-start | bytes 8388608 | tf_op jit(solution)/shard_map/all_to_all | solution.py:50
  358.2 3.7 reshape.168
  366.7 38.1 %collective-permute-done.6 = f32[4352]{0:T(1024)S(1)} collective-permute-done((f32[4352]{0:T(1024)S(1)}, f32[4352]{0:T(1024)S(1)}, u32[]{:S(2)}, u32[]{:S(2)}) %collective-permute-start.6) | collective-permute-done | bytes 17440 | tf_op jit(solution)/shard_map/ppermute | solution.py:40
  404.9 3.8 collective-permute-done.7
  408.7 4.7 %collective-permute-done.8 = f32[4352]{0:T(1024)S(1)} collective-permute-done((f32[4352]{0:T(1024)S(1)}, f32[4352]{0:T(1024)S(1)}, u32[]{:S(2)}, u32[]{:S(2)}) %collective-permute-start.8) | collective-permute-done | bytes 17440 | tf_op jit(solution)/shard_map/ppermute | solution.py:40
  414.6 6.5 %collective-permute-done.9 = f32[4352]{0:T(1024)S(1)} collective-permute-done((f32[4352]{0:T(1024)S(1)}, f32[4352]{0:T(1024)S(1)}, u32[]{:S(2)}, u32[]{:S(2)}) %collective-permute-start.9) | collective-permute-done | bytes 17440 | tf_op jit(solution)/shard_map/ppermute | solution.py:40
  (171 shorter events, 87.5 us)
Async XLA Ops:
  7.2 97.5 %all-gather.4.cloned.1.call-start = ((), (), s32[]{:S(2)}) async-start(), calls=%async_computation.4 | async-start | bytes 4456448 | tf_op jit(solution)/shard_map/all_gather | solution.py:114
  11.1 140.1 %all-gather.6.cloned.1.call-start = ((), (), s32[]{:S(2)}) async-start(), calls=%async_computation.7 | async-start | bytes 4456448 | tf_op jit(solution)/shard_map/all_gather | solution.py:141
  11.9 5.7 %copy-start.23 = (f32[3,3,256]{2,1,0:T(4,128)S(1)}, f32[3,3,256]{2,1,0:T(4,128)}, u32[]{:S(2)}) copy-start(f32[3,3,256]{2,1,0:T(4,128)} %param.9) | copy-start | bytes 27652
  11.9 5.8 %copy-start.21 = (f32[128,16]{0,1:T(8,128)S(1)}, f32[128,16]{0,1:T(8,128)}, u32[]{:S(2)}) copy-start(f32[128,16]{0,1:T(8,128)} %param.10) | copy-start | bytes 24580
  11.9 417.8 %reduce-scatter.5.cloned.1.call-start = ((), (), s32[]{:S(2)}) async-start(), calls=%async_computation.6 | async-start | bytes 2228224 | tf_op jit(solution)/shard_map/reduce_scatter | solution.py:180
  15.2 85.4 %collective-permute-start = (bf16[2048,3,256]{0,2,1:T(8,128)(2,1)S(1)}, bf16[2048,3,256]{0,2,1:T(8,128)(2,1)}, u32[]{:S(2)}, u32[]{:S(2)}) collective-permute-start(bf16[2048,3,256]{0,2,1:T(8,128)(2,1)S(1)} %copy.36), channel_id=1, source_target_pairs={{0,128},{128,0},{1,129},{129,1},{2,130},{130,2},{3,131},{131,3},{4... | collective-permute-start | bytes 9437192 | tf_op jit(solution)/shard_map/ppermute | solution.py:20
  17.5 107.0 %collective-permute-start.3 = (bf16[256,2048]{1,0:T(8,128)(2,1)}, bf16[256,2048]{1,0:T(8,128)(2,1)}, u32[]{:S(2)}, u32[]{:S(2)}) collective-permute-start(bf16[256,2048]{1,0:T(8,128)(2,1)} %param.8), channel_id=1, source_target_pairs={{0,128},{128,0},{1,129},{129,1},{2,130},{130,2},{3,131},{131,3},{4... | collective-permute-start | bytes 3145736 | tf_op jit(solution)/shard_map/ppermute | solution.py:20
  112.2 15.0 %copy-start.9 = (bf16[512,768]{1,0:T(8,128)(2,1)}, bf16[512,768]{1,0:T(8,128)(2,1)S(1)}, u32[]{:S(2)}) copy-start(bf16[512,768]{1,0:T(8,128)(2,1)S(1)} %convolution_convert_fusion.3) | copy-start | bytes 2359300
  112.4 14.8 %collective-permute-start.1 = (bf16[2,3,256]{0,2,1:T(8,128)(2,1)S(1)}, bf16[2,3,256]{0,2,1:T(8,128)(2,1)S(1)}, u32[]{:S(2)}, u32[]{:S(2)}) collective-permute-start(bf16[2,3,256]{0,2,1:T(8,128)(2,1)S(1)} %bitcast.169), channel_id=1, source_target_pairs={{0,16},{16,32},{32,48},{48,64},{64,80},{80,96},{96,112},{1,17},{17... | collective-permute-start | bytes 9224 | tf_op jit(solution)/shard_map/ppermute | solution.py:12
  128.9 27.3 %copy-start.5 = (f32[512,3,256]{0,2,1:T(8,128)}, f32[512,3,256]{0,2,1:T(8,128)S(1)}, u32[]{:S(2)}) copy-start(f32[512,3,256]{0,2,1:T(8,128)S(1)} %multiply_add_fusion) | copy-start | bytes 4718596
  159.2 12.6 %copy-start.7 = (bf16[16,128,256]{2,1,0:T(8,128)(2,1)S(1)}, bf16[16,128,256]{2,1,0:T(8,128)(2,1)}, u32[]{:S(2)}) copy-start(bf16[16,128,256]{2,1,0:T(8,128)(2,1)} %get-tuple-element.20) | copy-start | bytes 3145732
  159.2 6.5 %collective-permute-start.4 = (bf16[127,256]{0,1:T(8,128)(2,1)}, bf16[127,256]{0,1:T(8,128)(2,1)S(1)}, u32[]{:S(2)}, u32[]{:S(2)}) collective-permute-start(bf16[127,256]{0,1:T(8,128)(2,1)} %slice.148), channel_id=1, source_target_pairs={{16,0},{32,16},{48,32},{64,48},{80,64},{96,80},{112,96},{17,1},{33... | collective-permute-start | bytes 195080 | tf_op jit(solution)/shard_map/ppermute | solution.py:12
  173.6 5.3 %copy-start = (f32[2,8,128,256]{3,2,1,0:T(8,128)S(1)}, f32[2,8,128,256]{3,2,1,0:T(8,128)}, u32[]{:S(2)}) copy-start(f32[2,8,128,256]{3,2,1,0:T(8,128)} %copy.63) | copy-start | bytes 6291460
  175.4 5.4 %collective-permute-start.2 = (bf16[127,256]{0,1:T(8,128)(2,1)S(1)}, bf16[127,256]{0,1:T(8,128)(2,1)S(1)}, u32[]{:S(2)}, u32[]{:S(2)}) collective-permute-start(bf16[127,256]{0,1:T(8,128)(2,1)S(1)} %slice_bitcast_fusion.1), channel_id=1, source_target_pairs={{0,16},{16,32},{32,48},{48,64},{64,80},{80,96},{96,112},{1,17},{17... | collective-permute-start | bytes 195080 | tf_op jit(solution)/shard_map/ppermute | solution.py:12
  194.0 235.7 %reduce-scatter.3.cloned.1.call-start = ((), (), s32[]{:S(2)}) async-start(), calls=%async_computation.5 | async-start | bytes 6684672 | tf_op jit(solution)/shard_map/reduce_scatter | solution.py:177
  194.2 11.5 %collective-permute-start.5 = (f32[2,3,256]{0,2,1:T(8,128)S(1)}, f32[2,3,256]{0,2,1:T(8,128)S(1)}, u32[]{:S(2)}, u32[]{:S(2)}) collective-permute-start(f32[2,3,256]{0,2,1:T(8,128)S(1)} %slice.151), channel_id=1, source_target_pairs={{16,0},{32,16},{48,32},{64,48},{80,64},{96,80},{112,96},{17,1},{33... | collective-permute-start | bytes 18440 | tf_op jit(solution)/shard_map/ppermute | solution.py:12
  221.5 4.9 %copy-start.18 = (bf16[512,3,256]{0,2,1:T(8,128)(2,1)S(1)}, bf16[512,3,256]{0,2,1:T(8,128)(2,1)}, u32[]{:S(2)}) copy-start(bf16[512,3,256]{0,2,1:T(8,128)(2,1)} %copy-done.17) | copy-start | bytes 2359300
  221.5 128.7 %all-to-all-start = ((bf16[16,32,4096]{2,1,0:T(8,128)(2,1)}), bf16[16,32,4096]{2,1,0:T(8,128)(2,1)}, u32[]{:S(2)}, u32[]{:S(2)}) async-start(bf16[16,32,4096]{2,1,0:T(8,128)(2,1)} %bitcast.157), calls=%async_computation | async-start | bytes 8388608 | tf_op jit(solution)/shard_map/all_to_all | solution.py:50
  350.3 4.7 %copy-start.11 = (bf16[4,128,16,16]{1,0,3,2:T(4,128)(2,1)S(1)}, bf16[4,128,16,16]{1,0,3,2:T(4,128)(2,1)}, u32[]{:S(2)}) copy-start(bf16[4,128,16,16]{1,0,3,2:T(4,128)(2,1)} %slice.126) | copy-start | bytes 786436
  350.3 75.2 %all-to-all-start.1 = ((bf16[16,32,4096]{2,1,0:T(8,128)(2,1)}), bf16[16,32,4096]{2,1,0:T(8,128)(2,1)}, u32[]{:S(2)}, u32[]{:S(2)}) async-start(bf16[16,32,4096]{2,1,0:T(8,128)(2,1)} %bitcast.165), calls=%async_computation.1 | async-start | bytes 8388608 | tf_op jit(solution)/shard_map/all_to_all | solution.py:50
  364.7 40.2 %collective-permute-start.6 = (f32[4352]{0:T(1024)S(1)}, f32[4352]{0:T(1024)S(1)}, u32[]{:S(2)}, u32[]{:S(2)}) collective-permute-start(f32[4352]{0:T(1024)S(1)} %constant_dynamic-update-slice_fusion.1), channel_id=1, source_target_pairs={{0,128},{128,0},{1,129},{129,1},{2,130},{130,2},{3,131},{131,3},{4... | collective-permute-start | bytes 52232 | tf_op jit(solution)/shard_map/ppermute | solution.py:40
  404.9 3.8 collective-permute-start.7
  408.7 4.7 %collective-permute-start.8 = (f32[4352]{0:T(1024)S(1)}, f32[4352]{0:T(1024)S(1)}, u32[]{:S(2)}, u32[]{:S(2)}) collective-permute-start(f32[4352]{0:T(1024)S(1)} %add.105), channel_id=1, source_target_pairs={{0,32},{16,48},{32,0},{48,16},{64,96},{80,112},{96,64},{112,80},{1... | collective-permute-start | bytes 52232 | tf_op jit(solution)/shard_map/ppermute | solution.py:40
  413.3 7.7 %collective-permute-start.9 = (f32[4352]{0:T(1024)S(1)}, f32[4352]{0:T(1024)S(1)}, u32[]{:S(2)}, u32[]{:S(2)}) collective-permute-start(f32[4352]{0:T(1024)S(1)} %add.106), channel_id=1, source_target_pairs={{0,64},{16,80},{32,96},{48,112},{64,0},{80,16},{96,32},{112,48},{1... | collective-permute-start | bytes 52232 | tf_op jit(solution)/shard_map/ppermute | solution.py:40
  (23 other events, 48.4 us)
Sparse Core Ops, SparseCore 0:
  11.3 76.3 all-gather.3
  90.5 60.7 all-gather.5
  194.1 75.2 reduce-scatter.4
  272.4 83.5 reduce-scatter.2

commit v3 on v2

--- a/solution.py
+++ b/solution.py
@@ -4,6 +4,7 @@
 from jax.sharding import PartitionSpec as P
 
 EPS = 1e-05
+TENSOR = ("tchip", "core")
 
 
 def from_behind(value, axis, steps):
@@ -43,6 +44,17 @@
     return value
 
 
+def pair_scatter_sum(value):
+    chips = lax.axis_size("tchip")
+    cores = lax.axis_size("core")
+    rows, width = value.shape
+    value = value.reshape(chips, cores, rows // (chips * cores), width)
+    pieces = lax.all_to_all(value, "core", 1, 1)
+    paired = jnp.sum(pieces.astype(jnp.float32), axis=1).astype(jnp.bfloat16)
+    pieces = lax.all_to_all(paired, "tchip", 0, 0)
+    return jnp.sum(pieces.astype(jnp.float32), axis=0)
+
+
 def scatter_sum(value, axis, dim):
     count = lax.axis_size(axis)
     shape = value.shape
@@ -103,7 +115,7 @@
 def per_device(activations, in_weight, out_weight, short_filter, mixer_filter, cotangent):
     rows_own = activations.shape[1]
     width = activations.shape[2]
-    rows = rows_own * lax.axis_size("tensor")
+    rows = rows_own * lax.axis_size("tchip") * lax.axis_size("core")
     span = mixer_filter.shape[0]
     groups = mixer_filter.shape[1]
     taps = short_filter.shape[1]
@@ -111,7 +123,7 @@
     own = activations[0].astype(jnp.float32)
     inverse = lax.rsqrt(jnp.mean(own * own, axis=-1, keepdims=True) + EPS)
     normed = (own * inverse).astype(jnp.bfloat16)
-    slab = lax.all_gather(normed, "tensor", axis=0, tiled=True)
+    slab = lax.all_gather(normed, TENSOR, axis=0, tiled=True)
     full_in = pair_gather(in_weight, "dp", 0)
     full_out = pair_gather(out_weight, "dp", 1)
     in_flat = full_in.reshape(width, 3 * chans)
@@ -132,13 +144,11 @@
     mixed = band_apply(table_fwd, gate_ext, span)
     output_rows = (streams[:, 0] * mixed).astype(jnp.bfloat16)
     piece = output_rows
-    branch = scatter_sum(
-        jnp.dot(piece, full_out, preferred_element_type=jnp.float32).astype(jnp.bfloat16),
-        "tensor",
-        0,
+    branch = pair_scatter_sum(
+        jnp.dot(piece, full_out, preferred_element_type=jnp.float32).astype(jnp.bfloat16)
     )
     block_out = (own + branch).astype(jnp.bfloat16)[None]
-    cot_slab = lax.all_gather(cotangent[0], "tensor", axis=0, tiled=True)
+    cot_slab = lax.all_gather(cotangent[0], TENSOR, axis=0, tiled=True)
     grad_rows = lax.dot_general(
         cot_slab, full_out, (((1,), (1,)), ((), ())), preferred_element_type=jnp.float32
     )
@@ -182,12 +192,10 @@
         ).astype(jnp.float32),
     )
     piece = proj_flat
-    grad_norm = scatter_sum(
+    grad_norm = pair_scatter_sum(
         lax.dot_general(
             piece, in_flat, (((1,), (1,)), ((), ())), preferred_element_type=jnp.float32
-        ).astype(jnp.bfloat16),
-        "tensor",
-        0,
+        ).astype(jnp.bfloat16)
     )
     grad_x = (
         cotangent[0].astype(jnp.float32)
@@ -206,25 +214,32 @@
 
 
 def solution(mesh):
+    devices = mesh.devices
+    lead = devices.shape[:2]
+    cores = 2
+    chips = devices.shape[2] // cores
+    mesh = jax.sharding.Mesh(
+        devices.reshape(lead + (chips, cores)), ("dp", "context", "tchip", "core")
+    )
     placed = (
-        P("dp", ("context", "tensor"), None),
-        P("dp", None, "tensor"),
-        P("tensor", "dp"),
-        P(None, None, "tensor"),
-        P(None, "tensor"),
-        P("dp", ("context", "tensor"), None),
+        P("dp", ("context", "tchip", "core"), None),
+        P("dp", None, TENSOR),
+        P(TENSOR, "dp"),
+        P(None, None, TENSOR),
+        P(None, TENSOR),
+        P("dp", ("context", "tchip", "core"), None),
     )
     return jax.shard_map(
         per_device,
         mesh=mesh,
         in_specs=placed,
         out_specs=(
-            P("dp", ("context", "tensor"), None),
-            P("dp", ("context", "tensor"), None),
-            P(("dp", "context"), None, "tensor"),
-            P("tensor", ("dp", "context")),
-            P(None, None, "tensor"),
-            P(None, "tensor"),
+            P("dp", ("context", "tchip", "core"), None),
+            P("dp", ("context", "tchip", "core"), None),
+            P(("dp", "context"), None, TENSOR),
+            P(TENSOR, ("dp", "context")),
+            P(None, None, TENSOR),
+            P(None, TENSOR),
         ),
         check_vma=False,
     )

time: 438 us -> 404 us (0.922)
  waiting for transfers between devices: 269 us -> 209 us
  blocking collectives: 0 us -> 16.3 us
  other arithmetic: 26.5 us -> 34.1 us
  local copies, waits for them, and re-layouts: 62.7 us -> 67.8 us
    all_to_all x2, waiting for transfers between devices: 116 us -> 26.8 us  [pair_scatter_sum(): pieces = lax.all_to_all(paired, 'tchip', 0, 0)]
    ppermute x4, waiting for transfers between devices: 53.1 us -> 83.2 us  [tree_psum(): partner = lax.ppermute(value, axis, [(i, i ^ step) for i in range(count)])]
    all_to_all x0 -> x2, blocking collectives: none -> 16.3 us  [pair_scatter_sum(): pieces = lax.all_to_all(value, 'core', 1, 1)]
    reduce_sum x2 -> x4, other arithmetic: 6.02 us -> 14.1 us  [the longest x2 10.1 us: pair_scatter_sum(): paired = jnp.sum(pieces.astype(jnp.float32), axis=1).astype(jnp.bfloat16)]
    unnamed x68 -> x70, local copies, waits for them, and re-layouts: 15.4 us -> 17.2 us
  transfers between devices with their start and end apart: 16 -> 16, of which waited for: 11 -> 11; matrix products, arithmetic and copies ran while one was open for 20% -> 23% of each run, Pallas kernels for 0% -> 0%
where the time goes in v3:
time: 404 us; the launch traced here: 401 us
  waiting for transfers between devices  209 us (52%)
  local copies, waits for them, and re-layouts  67.8 us (17%)
  matrix products  34.8 us (9%)
  other arithmetic  34.1 us (8%)
  starting transfers between devices  24.3 us (6%)
  blocking collectives  16.3 us (4%)
  between operations  14.4 us (4%)
    ppermute x4, waiting for transfers between devices, tree_psum(): partner = lax.ppermute(value, axis, [(i, i ^ step) for i in range(count)])  83.2 us
    ppermute x2, waiting for transfers between devices, pair_gather(): lax.ppermute(value, axis, [(i, (i + step) % count) for i in range(count)])  61.9 us
    all_to_all x2, waiting for transfers between devices, pair_scatter_sum(): pieces = lax.all_to_all(paired, 'tchip', 0, 0)  26.8 us
    all_gather x1, waiting for transfers between devices, per_device(): cot_slab = lax.all_gather(cotangent[0], TENSOR, axis=0, tiled=True)  22.3 us
    unnamed x70, local copies, waits for them, and re-layouts  17.2 us
    all_to_all x2, blocking collectives, pair_scatter_sum(): pieces = lax.all_to_all(value, 'core', 1, 1)  16.3 us
    ppermute x4, waiting for transfers between devices, from_behind(): lax.ppermute(value, axis, [(source, source + steps) for source in range(i...  14.1 us
    another operation x4, local copies, waits for them, and re-layouts, skew_table(): jnp.tile(padded[:, None, :], (1, span, 1))  11.6 us
  transfers between devices with their start and end apart: 16, of which 11 were waited for; matrix products, arithmetic and copies ran while one was open for 23% of the time, Pallas kernels for 0%

profile of v3, /device:TPU:2, one launch (start us, length us, event | category | flops | bytes accessed | tf_op | source)
XLA Modules:
  0.0 400.8 jit_solution(4540653505624320499)
XLA Ops:
  19.7 3.9 tile.17
  29.1 3.9 tile.15
  47.0 53.7 %collective-permute-done = bf16[2048,3,256]{0,2,1:T(8,128)(2,1)} collective-permute-done((bf16[2048,3,256]{0,2,1:T(8,128)(2,1)S(1)}, bf16[2048,3,256]{0,2,1:T(8,128)(2,1)}, u32[]{:S(2)}, u32[]{:S(2)}) %collective-permute-start) | collective-permute-done | bytes 3145760 | tf_op jit(solution)/shard_map/ppermute | solution.py:21
  100.7 4.2 %constant_dynamic-update-slice_fusion.4 = bf16[4096,3,256]{0,2,1:T(8,128)(2,1)} fusion(bf16[4096,3,256]{0,2,1:T(8,128)(2,1)} %constant_dynamic-update-slice_fusion.5, bf16[2048,3,256]{0,2,1:T(8,128)(2,1)} %collective-permute-done, s32[]{:T(128)S(6)} %select_n.26), kind=kLoop, calls=%fused_computation.90 | loop fusion | bytes 6291460 | tf_op jit(solution)/shard_map/dynamic_update_slice | solution.py:29
  104.9 7.5 %convolution_convert_fusion.3 = bf16[512,768]{1,0:T(8,128)(2,1)S(1)} fusion(bf16[512,4096]{1,0:T(8,128)(2,1)} %all-gather.4.cloned.1.call-done, bf16[4096,768]{0,1:T(8,128)(2,1)} %bitcast.1), kind=kOutput, calls=%fused_computation.31 | convolution fusion | flops 3221618688 | bytes 11272192 | tf_op jit(solution)/shard_map/dot_general | solution.py:131
  112.6 3.8 collective-permute-start.1
  116.4 8.2 %collective-permute-done.3 = bf16[256,2048]{1,0:T(8,128)(2,1)} collective-permute-done((bf16[256,2048]{1,0:T(8,128)(2,1)}, bf16[256,2048]{1,0:T(8,128)(2,1)}, u32[]{:S(2)}, u32[]{:S(2)}) %collective-permute-start.3) | collective-permute-done | bytes 1048608 | tf_op jit(solution)/shard_map/ppermute | solution.py:21
  129.0 22.3 %all-gather.6.cloned.1.call-done = bf16[1,512,4096]{2,1,0:T(8,128)(2,1)} async-done(((bf16[1,32,4096]{2,1,0:T(8,128)(2,1)}), bf16[1,512,4096]{2,1,0:T(8,128)(2,1)}) %all-gather.6.cloned.1.call-update) | async-done | bytes 4194320 | tf_op jit(solution)/shard_map/all_gather | solution.py:151
  151.3 5.0 %multiply_convert_fusion = (bf16[512,256]{0,1:T(8,128)(2,1)}, f32[512,256]{0,1:T(8,128)}) fusion(f32[512,3,256]{0,2,1:T(8,128)S(1)} %multiply_add_fusion, bf16[256,4096]{1,0:T(8,128)(2,1)} %constant_dynamic-update-slice_fusion.2, bf16[1,512,4096]{2,1,0:T(8,128)(2,1)} %all-gather.6.cloned.1.call-done), kind=kOutput, calls=%fused_computation.64 | convolution fusion | flops 1074003968 | bytes 7602176 | tf_op jit(solution)/shard_map/dot_general | solution.py:152
  161.3 3.9 collective-permute-done.4
  197.1 10.0 %collective-permute-done.5 = f32[2,3,256]{0,2,1:T(8,128)S(1)} collective-permute-done((f32[2,3,256]{0,2,1:T(8,128)S(1)}, f32[2,3,256]{0,2,1:T(8,128)S(1)}, u32[]{:S(2)}, u32[]{:S(2)}) %collective-permute-start.5) | collective-permute-done | bytes 6176 | tf_op jit(solution)/shard_map/ppermute | solution.py:13
  211.6 5.4 %convolution_convert_fusion = bf16[4096,3,256]{2,0,1:T(8,128)(2,1)} fusion(bf16[512,4096]{1,0:T(8,128)(2,1)S(1)} %copy-done.28, bf16[512,3,256]{0,2,1:T(8,128)(2,1)S(1)} %get-tuple-element.32), kind=kOutput, calls=%fused_computation.1 | convolution fusion | flops 3224371200 | bytes 11272192 | tf_op jit(solution)/shard_map/dot_general | solution.py:183
  221.3 8.1 %all_to_all.20 = bf16[8,2,32,4096]{3,2,0,1:T(8,128)(2,1)} all-to-all(bf16[8,2,32,4096]{3,2,0,1:T(8,128)(2,1)S(1)} %copy.61), channel_id=1, replica_groups=mesh['dp'=2,'context'=8,'tchip'=8,'core'=2] {'core'}, dimensions={1} | all-to-all | bytes 8388608 | tf_op jit(solution)/shard_map/all_to_all | solution.py:52
  229.4 5.1 %reduce_sum.101 = bf16[8,32,4096]{2,1,0:T(8,128)(2,1)} reduce(bf16[8,2,32,4096]{3,2,0,1:T(8,128)(2,1)} %all_to_all.20, bf16[]{:T(256)} %constant.43.clone.1), dimensions={1}, to_apply=%region_1.2 | reduce | flops 1048576 | bytes 6291458 | tf_op jit(solution)/shard_map/reduce_sum | solution.py:53
  234.5 6.5 %bitcast_convert_fusion = bf16[512,4096]{1,0:T(8,128)(2,1)S(1)} fusion(bf16[512,3,256]{0,2,1:T(8,128)(2,1)S(1)} %copy-done.19, bf16[4096,3,256]{0,2,1:T(8,128)(2,1)} %constant_dynamic-update-slice_fusion.4), kind=kOutput, calls=%fused_computation | convolution fusion | flops 3223322624 | bytes 11272192 | tf_op jit(solution)/shard_map/dot_general | solution.py:196
  241.5 8.2 %all_to_all.21 = bf16[8,2,32,4096]{3,2,0,1:T(8,128)(2,1)} all-to-all(bf16[8,2,32,4096]{3,2,0,1:T(8,128)(2,1)S(1)} %copy.67), channel_id=1, replica_groups=mesh['dp'=2,'context'=8,'tchip'=8,'core'=2] {'core'}, dimensions={1} | all-to-all | bytes 8388608 | tf_op jit(solution)/shard_map/all_to_all | solution.py:52
  253.4 5.1 %reduce_sum.104 = bf16[8,32,4096]{2,1,0:T(8,128)(2,1)} reduce(bf16[8,2,32,4096]{3,2,0,1:T(8,128)(2,1)} %all_to_all.21, bf16[]{:T(256)} %constant.43.clone.1), dimensions={1}, to_apply=%region_3.4 | reduce | flops 1048576 | bytes 6291458 | tf_op jit(solution)/shard_map/reduce_sum | solution.py:53
  258.4 26.8 %all-to-all-done.1 = bf16[8,32,4096]{2,1,0:T(8,128)(2,1)S(1)} async-done(((bf16[8,32,4096]{2,1,0:T(8,128)(2,1)}), bf16[8,32,4096]{2,1,0:T(8,128)(2,1)S(1)}, u32[]{:S(2)}, u32[]{:S(2)}) %all-to-all-start.1) | async-done | bytes 2097184 | tf_op jit(solution)/shard_map/all_to_all | solution.py:54
  286.6 4.6 %all-to-all-start.3 = ((bf16[8,32,4096]{2,1,0:T(8,128)(2,1)}), bf16[8,32,4096]{2,1,0:T(8,128)(2,1)}, u32[]{:S(2)}, u32[]{:S(2)}) async-start(bf16[8,32,4096]{2,1,0:T(8,128)(2,1)} %reduce_sum.104), calls=%async_computation.3 | async-start | bytes 4194304 | tf_op jit(solution)/shard_map/all_to_all | solution.py:54
  296.8 3.7 reshape.168
  302.9 68.6 %collective-permute-done.6 = f32[4352]{0:T(1024)S(1)} collective-permute-done((f32[4352]{0:T(1024)S(1)}, f32[4352]{0:T(1024)S(1)}, u32[]{:S(2)}, u32[]{:S(2)}) %collective-permute-start.6) | collective-permute-done | bytes 17440 | tf_op jit(solution)/shard_map/ppermute | solution.py:41
  371.5 3.8 collective-permute-done.7
  375.3 4.7 %collective-permute-done.8 = f32[4352]{0:T(1024)S(1)} collective-permute-done((f32[4352]{0:T(1024)S(1)}, f32[4352]{0:T(1024)S(1)}, u32[]{:S(2)}, u32[]{:S(2)}) %collective-permute-start.8) | collective-permute-done | bytes 17440 | tf_op jit(solution)/shard_map/ppermute | solution.py:41
  381.5 6.2 %collective-permute-done.9 = f32[4352]{0:T(1024)S(1)} collective-permute-done((f32[4352]{0:T(1024)S(1)}, f32[4352]{0:T(1024)S(1)}, u32[]{:S(2)}, u32[]{:S(2)}) %collective-permute-start.9) | collective-permute-done | bytes 17440 | tf_op jit(solution)/shard_map/ppermute | solution.py:41
  (179 shorter events, 103.3 us)
Async XLA Ops:
  7.2 97.7 %all-gather.4.cloned.1.call-start = ((), (), s32[]{:S(2)}) async-start(), calls=%async_computation.6 | async-start | bytes 4456448 | tf_op jit(solution)/shard_map/all_gather | solution.py:126
  11.2 140.1 %all-gather.6.cloned.1.call-start = ((), (), s32[]{:S(2)}) async-start(), calls=%async_computation.9 | async-start | bytes 4456448 | tf_op jit(solution)/shard_map/all_gather | solution.py:151
  11.9 5.7 %copy-start.24 = (f32[3,3,256]{2,1,0:T(4,128)S(1)}, f32[3,3,256]{2,1,0:T(4,128)}, u32[]{:S(2)}) copy-start(f32[3,3,256]{2,1,0:T(4,128)} %param.9) | copy-start | bytes 27652
  12.0 5.8 %copy-start.22 = (f32[128,16]{0,1:T(8,128)S(1)}, f32[128,16]{0,1:T(8,128)}, u32[]{:S(2)}) copy-start(f32[128,16]{0,1:T(8,128)} %param.10) | copy-start | bytes 24580
  12.0 382.3 %reduce-scatter.5.cloned.1.call-start = ((), (), s32[]{:S(2)}) async-start(), calls=%async_computation.8 | async-start | bytes 2228224 | tf_op jit(solution)/shard_map/reduce_scatter | solution.py:190
  15.2 85.4 %collective-permute-start = (bf16[2048,3,256]{0,2,1:T(8,128)(2,1)S(1)}, bf16[2048,3,256]{0,2,1:T(8,128)(2,1)}, u32[]{:S(2)}, u32[]{:S(2)}) collective-permute-start(bf16[2048,3,256]{0,2,1:T(8,128)(2,1)S(1)} %copy.54), channel_id=1, source_target_pairs={{0,128},{128,0},{1,129},{129,1},{2,130},{130,2},{3,131},{131,3},{4... | collective-permute-start | bytes 9437192 | tf_op jit(solution)/shard_map/ppermute | solution.py:21
  17.6 107.0 %collective-permute-start.3 = (bf16[256,2048]{1,0:T(8,128)(2,1)}, bf16[256,2048]{1,0:T(8,128)(2,1)}, u32[]{:S(2)}, u32[]{:S(2)}) collective-permute-start(bf16[256,2048]{1,0:T(8,128)(2,1)} %param.8), channel_id=1, source_target_pairs={{0,128},{128,0},{1,129},{129,1},{2,130},{130,2},{3,131},{131,3},{4... | collective-permute-start | bytes 3145736 | tf_op jit(solution)/shard_map/ppermute | solution.py:21
  112.4 14.9 %copy-start.10 = (bf16[512,768]{1,0:T(8,128)(2,1)}, bf16[512,768]{1,0:T(8,128)(2,1)S(1)}, u32[]{:S(2)}) copy-start(bf16[512,768]{1,0:T(8,128)(2,1)S(1)} %convolution_convert_fusion.3) | copy-start | bytes 2359300
  112.6 14.7 %collective-permute-start.1 = (bf16[2,3,256]{0,2,1:T(8,128)(2,1)S(1)}, bf16[2,3,256]{0,2,1:T(8,128)(2,1)S(1)}, u32[]{:S(2)}, u32[]{:S(2)}) collective-permute-start(bf16[2,3,256]{0,2,1:T(8,128)(2,1)S(1)} %bitcast.169), channel_id=1, source_target_pairs={{0,16},{16,32},{32,48},{48,64},{64,80},{80,96},{96,112},{1,17},{17... | collective-permute-start | bytes 9224 | tf_op jit(solution)/shard_map/ppermute | solution.py:13
  129.0 27.3 %copy-start.6 = (f32[512,3,256]{0,2,1:T(8,128)}, f32[512,3,256]{0,2,1:T(8,128)S(1)}, u32[]{:S(2)}) copy-start(f32[512,3,256]{0,2,1:T(8,128)S(1)} %multiply_add_fusion) | copy-start | bytes 4718596
  158.8 12.4 %copy-start.8 = (bf16[16,128,256]{2,1,0:T(8,128)(2,1)S(1)}, bf16[16,128,256]{2,1,0:T(8,128)(2,1)}, u32[]{:S(2)}) copy-start(bf16[16,128,256]{2,1,0:T(8,128)(2,1)} %get-tuple-element.26) | copy-start | bytes 3145732
  158.8 6.3 %collective-permute-start.4 = (bf16[127,256]{0,1:T(8,128)(2,1)S(1)}, bf16[127,256]{0,1:T(8,128)(2,1)S(1)}, u32[]{:S(2)}, u32[]{:S(2)}) collective-permute-start(bf16[127,256]{0,1:T(8,128)(2,1)S(1)} %slice.148), channel_id=1, source_target_pairs={{16,0},{32,16},{48,32},{64,48},{80,64},{96,80},{112,96},{17,1},{33... | collective-permute-start | bytes 195080 | tf_op jit(solution)/shard_map/ppermute | solution.py:13
  173.0 5.3 %copy-start.1 = (f32[2,8,128,256]{3,2,1,0:T(8,128)S(1)}, f32[2,8,128,256]{3,2,1,0:T(8,128)}, u32[]{:S(2)}) copy-start(f32[2,8,128,256]{3,2,1,0:T(8,128)} %copy.83) | copy-start | bytes 6291460
  174.7 5.5 %copy-start.12 = (bf16[512,1,256]{0,2,1:T(8,128)(2,1)}, bf16[512,1,256]{0,2,1:T(8,128)(2,1)S(1)}, u32[]{:S(2)}) copy-start(bf16[512,1,256]{0,2,1:T(8,128)(2,1)S(1)} %get-tuple-element.33) | copy-start | bytes 786436
  174.8 5.4 %collective-permute-start.2 = (bf16[127,256]{0,1:T(8,128)(2,1)S(1)}, bf16[127,256]{0,1:T(8,128)(2,1)S(1)}, u32[]{:S(2)}, u32[]{:S(2)}) collective-permute-start(bf16[127,256]{0,1:T(8,128)(2,1)S(1)} %slice_bitcast_fusion.1), channel_id=1, source_target_pairs={{0,16},{16,32},{32,48},{48,64},{64,80},{80,96},{96,112},{1,17},{17... | collective-permute-start | bytes 195080 | tf_op jit(solution)/shard_map/ppermute | solution.py:13
  195.3 199.0 %reduce-scatter.3.cloned.1.call-start = ((), (), s32[]{:S(2)}) async-start(), calls=%async_computation.7 | async-start | bytes 6684672 | tf_op jit(solution)/shard_map/reduce_scatter | solution.py:187
  195.6 11.5 %collective-permute-start.5 = (f32[2,3,256]{0,2,1:T(8,128)S(1)}, f32[2,3,256]{0,2,1:T(8,128)S(1)}, u32[]{:S(2)}, u32[]{:S(2)}) collective-permute-start(f32[2,3,256]{0,2,1:T(8,128)S(1)} %slice.151), channel_id=1, source_target_pairs={{16,0},{32,16},{48,32},{64,48},{80,64},{96,80},{112,96},{17,1},{33... | collective-permute-start | bytes 18440 | tf_op jit(solution)/shard_map/ppermute | solution.py:13
  229.4 5.1 %copy-start.19 = (bf16[512,3,256]{0,2,1:T(8,128)(2,1)S(1)}, bf16[512,3,256]{0,2,1:T(8,128)(2,1)}, u32[]{:S(2)}) copy-start(bf16[512,3,256]{0,2,1:T(8,128)(2,1)} %copy-done.18) | copy-start | bytes 2359300
  249.7 35.6 %all-to-all-start.1 = ((bf16[8,32,4096]{2,1,0:T(8,128)(2,1)}), bf16[8,32,4096]{2,1,0:T(8,128)(2,1)S(1)}, u32[]{:S(2)}, u32[]{:S(2)}) async-start(bf16[8,32,4096]{2,1,0:T(8,128)(2,1)} %reduce_sum.101), calls=%async_computation.1 | async-start | bytes 4194304 | tf_op jit(solution)/shard_map/all_to_all | solution.py:54
  286.6 104.5 %all-to-all-start.3 = ((bf16[8,32,4096]{2,1,0:T(8,128)(2,1)}), bf16[8,32,4096]{2,1,0:T(8,128)(2,1)}, u32[]{:S(2)}, u32[]{:S(2)}) async-start(bf16[8,32,4096]{2,1,0:T(8,128)(2,1)} %reduce_sum.104), calls=%async_computation.3 | async-start | bytes 4194304 | tf_op jit(solution)/shard_map/all_to_all | solution.py:54
  301.2 70.3 %collective-permute-start.6 = (f32[4352]{0:T(1024)S(1)}, f32[4352]{0:T(1024)S(1)}, u32[]{:S(2)}, u32[]{:S(2)}) collective-permute-start(f32[4352]{0:T(1024)S(1)} %constant_dynamic-update-slice_fusion.1), channel_id=1, source_target_pairs={{0,128},{128,0},{1,129},{129,1},{2,130},{130,2},{3,131},{131,3},{4... | collective-permute-start | bytes 52232 | tf_op jit(solution)/shard_map/ppermute | solution.py:41
  371.5 3.8 collective-permute-start.7
  375.3 4.7 %collective-permute-start.8 = (f32[4352]{0:T(1024)S(1)}, f32[4352]{0:T(1024)S(1)}, u32[]{:S(2)}, u32[]{:S(2)}) collective-permute-start(f32[4352]{0:T(1024)S(1)} %add.105), channel_id=1, source_target_pairs={{0,32},{16,48},{32,0},{48,16},{64,96},{80,112},{96,64},{112,80},{1... | collective-permute-start | bytes 52232 | tf_op jit(solution)/shard_map/ppermute | solution.py:41
  380.0 7.7 %collective-permute-start.9 = (f32[4352]{0:T(1024)S(1)}, f32[4352]{0:T(1024)S(1)}, u32[]{:S(2)}, u32[]{:S(2)}) collective-permute-start(f32[4352]{0:T(1024)S(1)} %add.106), channel_id=1, source_target_pairs={{0,64},{16,80},{32,96},{48,112},{64,0},{80,16},{96,32},{112,48},{1... | collective-permute-start | bytes 52232 | tf_op jit(solution)/shard_map/ppermute | solution.py:41
  (24 other events, 46.0 us)
Sparse Core Ops, SparseCore 0:
  11.3 76.3 all-gather.3
  90.5 60.7 all-gather.5
  195.4 74.9 reduce-scatter.4
  273.4 83.9 reduce-scatter.2

commit v4 on v3

--- a/solution.py
+++ b/solution.py
@@ -187,9 +187,7 @@
         lax.psum_scatter(
             in_term.astype(jnp.bfloat16), ("dp", "context"), scatter_dimension=0, tiled=True
         ).astype(jnp.float32),
-        lax.psum_scatter(
-            out_term.astype(jnp.bfloat16), ("dp", "context"), scatter_dimension=1, tiled=True
-        ).astype(jnp.float32),
+        scatter_sum(out_term.astype(jnp.bfloat16), ("dp", "context"), 1),
     )
     piece = proj_flat
     grad_norm = pair_scatter_sum(

time: 404 us -> 444 us (1.099); the launches traced: 401 us -> 435 us
  waiting for transfers between devices: 209 us -> 225 us
  starting transfers between devices: 24.3 us -> 35.7 us
    all_to_all x2, waiting for transfers between devices: 26.8 us -> 86.8 us  [pair_scatter_sum(): pieces = lax.all_to_all(paired, 'tchip', 0, 0)]
    ppermute x4, waiting for transfers between devices: 83.2 us -> 39.3 us  [tree_psum(): partner = lax.ppermute(value, axis, [(i, i ^ step) for i in range(count)])]
    all_to_all x0 -> x1, starting transfers between devices: none -> 5.77 us  [scatter_sum(): pieces = lax.all_to_all(value.reshape(split), axis, dim, 0)]
    ppermute x4, starting transfers between devices: 3.2 us -> 8.97 us  [tree_psum(): partner = lax.ppermute(value, axis, [(i, i ^ step) for i in range(count)])]
    unnamed x70 -> x65, local copies, waits for them, and re-layouts: 17.2 us -> 17.3 us
  transfers between devices with their start and end apart: 16 -> 16, of which waited for: 11 -> 12; matrix products, arithmetic and copies ran while one was open for 23% -> 22% of each run, Pallas kernels for 0% -> 0%
where the time goes in v4:
time: 444 us; the launch traced here: 435 us
  waiting for transfers between devices  225 us (51%)
  local copies, waits for them, and re-layouts  69.3 us (16%)
  other arithmetic  38.3 us (9%)
  starting transfers between devices  35.7 us (8%)
  matrix products  35.6 us (8%)
  blocking collectives  16.5 us (4%)
  between operations  14.6 us (3%)
    all_to_all x2, waiting for transfers between devices, pair_scatter_sum(): pieces = lax.all_to_all(paired, 'tchip', 0, 0)  86.8 us
    ppermute x2, waiting for transfers between devices, pair_gather(): lax.ppermute(value, axis, [(i, (i + step) % count) for i in range(count)])  61.7 us
    ppermute x4, waiting for transfers between devices, tree_psum(): partner = lax.ppermute(value, axis, [(i, i ^ step) for i in range(count)])  39.3 us
    all_gather x1, waiting for transfers between devices, per_device(): cot_slab = lax.all_gather(cotangent[0], TENSOR, axis=0, tiled=True)  22.4 us
    unnamed x65, local copies, waits for them, and re-layouts  17.3 us
    all_to_all x2, blocking collectives, pair_scatter_sum(): pieces = lax.all_to_all(value, 'core', 1, 1)  16.5 us
    ppermute x4, waiting for transfers between devices, from_behind(): lax.ppermute(value, axis, [(source, source + steps) for source in range(i...  14.3 us
    another operation x4, local copies, waits for them, and re-layouts, skew_table(): jnp.tile(padded[:, None, :], (1, span, 1))  11.5 us
  transfers between devices with their start and end apart: 16, of which 12 were waited for; matrix products, arithmetic and copies ran while one was open for 22% of the time, Pallas kernels for 0%

profile of v4, /device:TPU:2, one launch (start us, length us, event | category | flops | bytes accessed | tf_op | source)
XLA Modules:
  0.0 435.3 jit_solution(2624497369891020172)
XLA Ops:
  19.8 3.9 tile.17
  29.2 3.9 tile.15
  47.0 53.8 %collective-permute-done = bf16[2048,3,256]{0,2,1:T(8,128)(2,1)} collective-permute-done((bf16[2048,3,256]{0,2,1:T(8,128)(2,1)S(1)}, bf16[2048,3,256]{0,2,1:T(8,128)(2,1)}, u32[]{:S(2)}, u32[]{:S(2)}) %collective-permute-start) | collective-permute-done | bytes 3145760 | tf_op jit(solution)/shard_map/ppermute | solution.py:21
  100.7 4.2 constant_dynamic-update-slice_fusion.4
  104.9 7.5 %convolution_convert_fusion.3 = bf16[512,768]{1,0:T(8,128)(2,1)S(1)} fusion(bf16[512,4096]{1,0:T(8,128)(2,1)} %all-gather.4.cloned.1.call-done, bf16[4096,768]{0,1:T(8,128)(2,1)} %bitcast.1), kind=kOutput, calls=%fused_computation.31 | convolution fusion | flops 3221618688 | bytes 11272192 | tf_op jit(solution)/shard_map/dot_general | solution.py:131
  112.7 4.1 collective-permute-start.1
  116.7 7.9 %collective-permute-done.3 = bf16[256,2048]{1,0:T(8,128)(2,1)} collective-permute-done((bf16[256,2048]{1,0:T(8,128)(2,1)}, bf16[256,2048]{1,0:T(8,128)(2,1)}, u32[]{:S(2)}, u32[]{:S(2)}) %collective-permute-start.3) | collective-permute-done | bytes 1048608 | tf_op jit(solution)/shard_map/ppermute | solution.py:21
  129.0 22.4 %all-gather.6.cloned.1.call-done = bf16[1,512,4096]{2,1,0:T(8,128)(2,1)} async-done(((bf16[1,32,4096]{2,1,0:T(8,128)(2,1)}), bf16[1,512,4096]{2,1,0:T(8,128)(2,1)}) %all-gather.6.cloned.1.call-update) | async-done | bytes 4194320 | tf_op jit(solution)/shard_map/all_gather | solution.py:151
  151.4 5.0 %multiply_convert_fusion = (bf16[512,256]{0,1:T(8,128)(2,1)}, f32[512,256]{0,1:T(8,128)}) fusion(f32[512,3,256]{0,2,1:T(8,128)S(1)} %multiply_add_fusion, bf16[256,4096]{1,0:T(8,128)(2,1)} %constant_dynamic-update-slice_fusion.2, bf16[1,512,4096]{2,1,0:T(8,128)(2,1)} %all-gather.6.cloned.1.call-done), kind=kOutput, calls=%fused_computation.64 | convolution fusion | flops 1074003968 | bytes 7602176 | tf_op jit(solution)/shard_map/dot_general | solution.py:152
  161.3 3.9 collective-permute-done.4
  193.6 10.2 %collective-permute-done.5 = f32[2,3,256]{0,2,1:T(8,128)S(1)} collective-permute-done((f32[2,3,256]{0,2,1:T(8,128)S(1)}, f32[2,3,256]{0,2,1:T(8,128)S(1)}, u32[]{:S(2)}, u32[]{:S(2)}) %collective-permute-start.5) | collective-permute-done | bytes 6176 | tf_op jit(solution)/shard_map/ppermute | solution.py:13
  208.4 5.4 %convolution_convert_fusion = bf16[4096,3,256]{2,0,1:T(8,128)(2,1)} fusion(bf16[512,4096]{1,0:T(8,128)(2,1)S(1)} %copy-done.26, bf16[512,3,256]{0,2,1:T(8,128)(2,1)S(1)} %get-tuple-element.32), kind=kOutput, calls=%fused_computation.1 | convolution fusion | flops 3224371200 | bytes 11272192 | tf_op jit(solution)/shard_map/dot_general | solution.py:183
  218.1 8.3 %all_to_all.29 = bf16[8,2,32,4096]{3,2,0,1:T(8,128)(2,1)} all-to-all(bf16[8,2,32,4096]{3,2,0,1:T(8,128)(2,1)S(1)} %copy.62), channel_id=1, replica_groups=mesh['dp'=2,'context'=8,'tchip'=8,'core'=2] {'core'}, dimensions={1} | all-to-all | bytes 8388608 | tf_op jit(solution)/shard_map/all_to_all | solution.py:52
  226.4 5.0 %reduce_sum.113 = bf16[8,32,4096]{2,1,0:T(8,128)(2,1)} reduce(bf16[8,2,32,4096]{3,2,0,1:T(8,128)(2,1)} %all_to_all.29, bf16[]{:T(256)} %constant.44.clone.1), dimensions={1}, to_apply=%region_1.2 | reduce | flops 1048576 | bytes 6291458 | tf_op jit(solution)/shard_map/reduce_sum | solution.py:53
  231.4 6.6 %bitcast_convert_fusion = bf16[512,4096]{1,0:T(8,128)(2,1)S(1)} fusion(bf16[512,3,256]{0,2,1:T(8,128)(2,1)S(1)} %copy-done.17, bf16[4096,3,256]{0,2,1:T(8,128)(2,1)} %constant_dynamic-update-slice_fusion.4), kind=kOutput, calls=%fused_computation | convolution fusion | flops 3223322624 | bytes 11272192 | tf_op jit(solution)/shard_map/dot_general | solution.py:194
  238.5 8.2 %all_to_all.30 = bf16[8,2,32,4096]{3,2,0,1:T(8,128)(2,1)} all-to-all(bf16[8,2,32,4096]{3,2,0,1:T(8,128)(2,1)S(1)} %copy.68), channel_id=1, replica_groups=mesh['dp'=2,'context'=8,'tchip'=8,'core'=2] {'core'}, dimensions={1} | all-to-all | bytes 8388608 | tf_op jit(solution)/shard_map/all_to_all | solution.py:52
  246.7 3.9 all-to-all-start.1
  250.5 5.1 %reduce_sum.116 = bf16[8,32,4096]{2,1,0:T(8,128)(2,1)} reduce(bf16[8,2,32,4096]{3,2,0,1:T(8,128)(2,1)} %all_to_all.30, bf16[]{:T(256)} %constant.44.clone.1), dimensions={1}, to_apply=%region_3.4 | reduce | flops 1048576 | bytes 6291458 | tf_op jit(solution)/shard_map/reduce_sum | solution.py:53
  255.6 64.0 %all-to-all-done.1 = bf16[8,32,4096]{2,1,0:T(8,128)(2,1)S(1)} async-done(((bf16[8,32,4096]{2,1,0:T(8,128)(2,1)}), bf16[8,32,4096]{2,1,0:T(8,128)(2,1)S(1)}, u32[]{:S(2)}, u32[]{:S(2)}) %all-to-all-start.1) | async-done | bytes 2097184 | tf_op jit(solution)/shard_map/all_to_all | solution.py:54
  321.0 4.4 all-to-all-start.3
  331.5 22.8 %all-to-all-done.3 = bf16[8,32,4096]{2,1,0:T(8,128)(2,1)} async-done(((bf16[8,32,4096]{2,1,0:T(8,128)(2,1)}), bf16[8,32,4096]{2,1,0:T(8,128)(2,1)}, u32[]{:S(2)}, u32[]{:S(2)}) %all-to-all-start.3) | async-done | bytes 2097184 | tf_op jit(solution)/shard_map/all_to_all | solution.py:54
  354.3 5.8 %all-to-all-start.4 = ((bf16[1,256,16,256]{3,1,0,2:T(8,128)(2,1)}), bf16[1,256,16,256]{3,1,0,2:T(8,128)(2,1)}, u32[]{:S(2)}, u32[]{:S(2)}) async-start(bf16[1,256,16,256]{3,1,0,2:T(8,128)(2,1)} %copy.69), calls=%async_computation.5 | async-start | bytes 4194304 | tf_op jit(solution)/shard_map/all_to_all | solution.py:62
  376.4 30.3 %collective-permute-done.7 = f32[4352]{0:T(1024)S(1)} collective-permute-done((f32[4352]{0:T(1024)S(1)}, f32[4352]{0:T(1024)S(1)}, u32[]{:S(2)}, u32[]{:S(2)}) %collective-permute-start.7) | collective-permute-done | bytes 17440 | tf_op jit(solution)/shard_map/ppermute | solution.py:41
  411.6 4.8 %collective-permute-start.9 = (f32[4352]{0:T(1024)S(1)}, f32[4352]{0:T(1024)S(1)}, u32[]{:S(2)}, u32[]{:S(2)}) collective-permute-start(f32[4352]{0:T(1024)S(1)} %add.104), channel_id=1, source_target_pairs={{0,64},{16,80},{32,96},{48,112},{64,0},{80,16},{96,32},{112,48},{1... | collective-permute-start | bytes 52232 | tf_op jit(solution)/shard_map/ppermute | solution.py:41
  (175 shorter events, 119.7 us)
Async XLA Ops:
  7.2 97.8 %all-gather.4.cloned.1.call-start = ((), (), s32[]{:S(2)}) async-start(), calls=%async_computation.6 | async-start | bytes 4456448 | tf_op jit(solution)/shard_map/all_gather | solution.py:126
  11.3 140.1 %all-gather.6.cloned.1.call-start = ((), (), s32[]{:S(2)}) async-start(), calls=%async_computation.8 | async-start | bytes 4456448 | tf_op jit(solution)/shard_map/all_gather | solution.py:151
  12.0 5.7 %copy-start.22 = (f32[3,3,256]{2,1,0:T(4,128)S(1)}, f32[3,3,256]{2,1,0:T(4,128)}, u32[]{:S(2)}) copy-start(f32[3,3,256]{2,1,0:T(4,128)} %param.9) | copy-start | bytes 27652
  12.0 5.8 %copy-start.20 = (f32[128,16]{0,1:T(8,128)S(1)}, f32[128,16]{0,1:T(8,128)}, u32[]{:S(2)}) copy-start(f32[128,16]{0,1:T(8,128)} %param.10) | copy-start | bytes 24580
  12.0 416.5 %reduce-scatter.2.cloned.1.call-start = ((), (), s32[]{:S(2)}) async-start(), calls=%async_computation.7 | async-start | bytes 6684672 | tf_op jit(solution)/shard_map/reduce_scatter | solution.py:187
  15.3 85.4 %collective-permute-start = (bf16[2048,3,256]{0,2,1:T(8,128)(2,1)S(1)}, bf16[2048,3,256]{0,2,1:T(8,128)(2,1)}, u32[]{:S(2)}, u32[]{:S(2)}) collective-permute-start(bf16[2048,3,256]{0,2,1:T(8,128)(2,1)S(1)} %copy.55), channel_id=1, source_target_pairs={{0,128},{128,0},{1,129},{129,1},{2,130},{130,2},{3,131},{131,3},{4... | collective-permute-start | bytes 9437192 | tf_op jit(solution)/shard_map/ppermute | solution.py:21
  17.6 107.0 %collective-permute-start.3 = (bf16[256,2048]{1,0:T(8,128)(2,1)}, bf16[256,2048]{1,0:T(8,128)(2,1)}, u32[]{:S(2)}, u32[]{:S(2)}) collective-permute-start(bf16[256,2048]{1,0:T(8,128)(2,1)} %param.8), channel_id=1, source_target_pairs={{0,128},{128,0},{1,129},{129,1},{2,130},{130,2},{3,131},{131,3},{4... | collective-permute-start | bytes 3145736 | tf_op jit(solution)/shard_map/ppermute | solution.py:21
  112.4 14.8 %copy-start.9 = (bf16[512,768]{1,0:T(8,128)(2,1)}, bf16[512,768]{1,0:T(8,128)(2,1)S(1)}, u32[]{:S(2)}) copy-start(bf16[512,768]{1,0:T(8,128)(2,1)S(1)} %convolution_convert_fusion.3) | copy-start | bytes 2359300
  112.7 14.6 %collective-permute-start.1 = (bf16[2,3,256]{0,2,1:T(8,128)(2,1)S(1)}, bf16[2,3,256]{0,2,1:T(8,128)(2,1)S(1)}, u32[]{:S(2)}, u32[]{:S(2)}) collective-permute-start(bf16[2,3,256]{0,2,1:T(8,128)(2,1)S(1)} %bitcast.174), channel_id=1, source_target_pairs={{0,16},{16,32},{32,48},{48,64},{64,80},{80,96},{96,112},{1,17},{17... | collective-permute-start | bytes 9224 | tf_op jit(solution)/shard_map/ppermute | solution.py:13
  129.0 27.4 %copy-start.5 = (f32[512,3,256]{0,2,1:T(8,128)}, f32[512,3,256]{0,2,1:T(8,128)S(1)}, u32[]{:S(2)}) copy-start(f32[512,3,256]{0,2,1:T(8,128)S(1)} %multiply_add_fusion) | copy-start | bytes 4718596
  158.9 12.4 %copy-start.7 = (bf16[16,128,256]{2,1,0:T(8,128)(2,1)S(1)}, bf16[16,128,256]{2,1,0:T(8,128)(2,1)}, u32[]{:S(2)}) copy-start(bf16[16,128,256]{2,1,0:T(8,128)(2,1)} %get-tuple-element.26) | copy-start | bytes 3145732
  158.9 6.3 %collective-permute-start.4 = (bf16[127,256]{0,1:T(8,128)(2,1)S(1)}, bf16[127,256]{0,1:T(8,128)(2,1)S(1)}, u32[]{:S(2)}, u32[]{:S(2)}) collective-permute-start(bf16[127,256]{0,1:T(8,128)(2,1)S(1)} %slice.148), channel_id=1, source_target_pairs={{16,0},{32,16},{48,32},{64,48},{80,64},{96,80},{112,96},{17,1},{33... | collective-permute-start | bytes 195080 | tf_op jit(solution)/shard_map/ppermute | solution.py:13
  173.1 5.3 %copy-start.1 = (f32[2,8,128,256]{3,2,1,0:T(8,128)S(1)}, f32[2,8,128,256]{3,2,1,0:T(8,128)}, u32[]{:S(2)}) copy-start(f32[2,8,128,256]{3,2,1,0:T(8,128)} %copy.85) | copy-start | bytes 6291460
  174.8 5.5 %copy-start.11 = (bf16[512,1,256]{0,2,1:T(8,128)(2,1)}, bf16[512,1,256]{0,2,1:T(8,128)(2,1)S(1)}, u32[]{:S(2)}) copy-start(bf16[512,1,256]{0,2,1:T(8,128)(2,1)S(1)} %get-tuple-element.33) | copy-start | bytes 786436
  174.9 5.4 %collective-permute-start.2 = (bf16[127,256]{0,1:T(8,128)(2,1)S(1)}, bf16[127,256]{0,1:T(8,128)(2,1)S(1)}, u32[]{:S(2)}, u32[]{:S(2)}) collective-permute-start(bf16[127,256]{0,1:T(8,128)(2,1)S(1)} %slice_bitcast_fusion.1), channel_id=1, source_target_pairs={{0,16},{16,32},{32,48},{48,64},{64,80},{80,96},{96,112},{1,17},{17... | collective-permute-start | bytes 195080 | tf_op jit(solution)/shard_map/ppermute | solution.py:13
  192.3 11.5 %collective-permute-start.5 = (f32[2,3,256]{0,2,1:T(8,128)S(1)}, f32[2,3,256]{0,2,1:T(8,128)S(1)}, u32[]{:S(2)}, u32[]{:S(2)}) collective-permute-start(f32[2,3,256]{0,2,1:T(8,128)S(1)} %slice.151), channel_id=1, source_target_pairs={{16,0},{32,16},{48,32},{64,48},{80,64},{96,80},{112,96},{17,1},{33... | collective-permute-start | bytes 18440 | tf_op jit(solution)/shard_map/ppermute | solution.py:13
  246.7 72.9 %all-to-all-start.1 = ((bf16[8,32,4096]{2,1,0:T(8,128)(2,1)}), bf16[8,32,4096]{2,1,0:T(8,128)(2,1)S(1)}, u32[]{:S(2)}, u32[]{:S(2)}) async-start(bf16[8,32,4096]{2,1,0:T(8,128)(2,1)} %reduce_sum.113), calls=%async_computation.1 | async-start | bytes 4194304 | tf_op jit(solution)/shard_map/all_to_all | solution.py:54
  321.0 33.3 %all-to-all-start.3 = ((bf16[8,32,4096]{2,1,0:T(8,128)(2,1)}), bf16[8,32,4096]{2,1,0:T(8,128)(2,1)}, u32[]{:S(2)}, u32[]{:S(2)}) async-start(bf16[8,32,4096]{2,1,0:T(8,128)(2,1)} %reduce_sum.116), calls=%async_computation.3 | async-start | bytes 4194304 | tf_op jit(solution)/shard_map/all_to_all | solution.py:54
  331.5 28.6 %copy-start.4 = (f32[512,3,256]{0,2,1:T(8,128)S(1)}, f32[512,3,256]{0,2,1:T(8,128)}, u32[]{:S(2)}) copy-start(f32[512,3,256]{0,2,1:T(8,128)} %copy-done.3) | copy-start | bytes 4718596
  354.3 71.7 %all-to-all-start.4 = ((bf16[1,256,16,256]{3,1,0,2:T(8,128)(2,1)}), bf16[1,256,16,256]{3,1,0,2:T(8,128)(2,1)}, u32[]{:S(2)}, u32[]{:S(2)}) async-start(bf16[1,256,16,256]{3,1,0,2:T(8,128)(2,1)} %copy.69), calls=%async_computation.5 | async-start | bytes 4194304 | tf_op jit(solution)/shard_map/all_to_all | solution.py:62
  371.1 3.9 collective-permute-start.6
  375.0 31.7 %collective-permute-start.7 = (f32[4352]{0:T(1024)S(1)}, f32[4352]{0:T(1024)S(1)}, u32[]{:S(2)}, u32[]{:S(2)}) collective-permute-start(f32[4352]{0:T(1024)S(1)} %add.102), channel_id=1, source_target_pairs={{0,16},{16,0},{32,48},{48,32},{64,80},{80,64},{96,112},{112,96},{1... | collective-permute-start | bytes 52232 | tf_op jit(solution)/shard_map/ppermute | solution.py:41
  406.7 4.9 %collective-permute-start.8 = (f32[4352]{0:T(1024)S(1)}, f32[4352]{0:T(1024)S(1)}, u32[]{:S(2)}, u32[]{:S(2)}) collective-permute-start(f32[4352]{0:T(1024)S(1)} %add.103), channel_id=1, source_target_pairs={{0,32},{16,48},{32,0},{48,16},{64,96},{80,112},{96,64},{112,80},{1... | collective-permute-start | bytes 52232 | tf_op jit(solution)/shard_map/ppermute | solution.py:41
  411.6 7.8 %collective-permute-start.9 = (f32[4352]{0:T(1024)S(1)}, f32[4352]{0:T(1024)S(1)}, u32[]{:S(2)}, u32[]{:S(2)}) collective-permute-start(f32[4352]{0:T(1024)S(1)} %add.104), channel_id=1, source_target_pairs={{0,64},{16,80},{32,96},{48,112},{64,0},{80,16},{96,32},{112,48},{1... | collective-permute-start | bytes 52232 | tf_op jit(solution)/shard_map/ppermute | solution.py:41
  (21 other events, 42.6 us)
Sparse Core Ops, SparseCore 0:
  11.4 76.3 all-gather.3
  90.6 60.7 all-gather.5
  213.9 87.1 reduce-scatter.1

commit v5 on v4

--- a/solution.py
+++ b/solution.py
@@ -153,7 +153,7 @@
         cot_slab, full_out, (((1,), (1,)), ((), ())), preferred_element_type=jnp.float32
     )
     out_term = lax.dot_general(
-        output_rows, cot_slab, (((0,), (0,)), ((), ())), preferred_element_type=jnp.float32
+        cot_slab, output_rows, (((0,), (0,)), ((), ())), preferred_element_type=jnp.float32
     )
     grad_mix = (grad_rows * streams[:, 0]).astype(jnp.bfloat16)
     grad_mix_wide = grad_mix.astype(jnp.float32)
@@ -183,12 +183,13 @@
     in_term = lax.dot_general(
         slab, proj_flat, (((0,), (0,)), ((), ())), preferred_element_type=jnp.float32
     ).reshape(width, 3, chans)
-    grad_in, grad_out = (
-        lax.psum_scatter(
-            in_term.astype(jnp.bfloat16), ("dp", "context"), scatter_dimension=0, tiled=True
-        ).astype(jnp.float32),
-        scatter_sum(out_term.astype(jnp.bfloat16), ("dp", "context"), 1),
-    )
+    in_cols = in_term.shape[1] * in_term.shape[2]
+    joined = jnp.concatenate(
+        [in_term.reshape(width, in_cols).astype(jnp.bfloat16), out_term.astype(jnp.bfloat16)], 1
+    )
+    joined = lax.psum_scatter(joined, ("dp", "context"), scatter_dimension=0, tiled=True)
+    grad_in = joined[:, :in_cols].reshape((-1,) + in_term.shape[1:])
+    grad_out = joined[:, in_cols:].T
     piece = proj_flat
     grad_norm = pair_scatter_sum(
         lax.dot_general(

time: 444 us -> 414 us (0.932); the launches traced: 435 us -> 412 us
  waiting for transfers between devices: 225 us -> 211 us
  starting transfers between devices: 35.7 us -> 22.9 us
    ppermute x4, waiting for transfers between devices: 39.3 us -> 30.3 us  [tree_psum(): partner = lax.ppermute(value, axis, [(i, i ^ step) for i in range(count)])]
    ppermute x4, starting transfers between devices: 8.97 us -> 1.64 us  [tree_psum(): partner = lax.ppermute(value, axis, [(i, i ^ step) for i in range(count)])]
    concatenate x0 -> x1, other arithmetic: none -> 7.14 us  [per_device(): jnp.concatenate([in_term.reshape(width, in_cols).astype(jnp.bfloat16), ou...]
    all_to_all x1 -> x0, starting transfers between devices: 5.77 us -> none  [scatter_sum(): pieces = lax.all_to_all(value.reshape(split), axis, dim, 0)]
    unnamed x65 -> x69, local copies, waits for them, and re-layouts: 17.3 us -> 18.8 us
  transfers between devices with their start and end apart: 16 -> 15, of which waited for: 12 -> 11; matrix products, arithmetic and copies ran while one was open for 22% -> 21% of each run, Pallas kernels for 0% -> 0%
where the time goes in v5:
time: 414 us; the launch traced here: 412 us
  waiting for transfers between devices  211 us (51%)
  local copies, waits for them, and re-layouts  71.3 us (17%)
  other arithmetic  41 us (10%)
  matrix products  34.8 us (8%)
  starting transfers between devices  22.9 us (6%)
  blocking collectives  16.4 us (4%)
  between operations  14.3 us (3%)
    all_to_all x2, waiting for transfers between devices, pair_scatter_sum(): pieces = lax.all_to_all(paired, 'tchip', 0, 0)  83.9 us
    ppermute x2, waiting for transfers between devices, pair_gather(): lax.ppermute(value, axis, [(i, (i + step) % count) for i in range(count)])  62.2 us
    ppermute x4, waiting for transfers between devices, tree_psum(): partner = lax.ppermute(value, axis, [(i, i ^ step) for i in range(count)])  30.3 us
    all_gather x1, waiting for transfers between devices, per_device(): cot_slab = lax.all_gather(cotangent[0], TENSOR, axis=0, tiled=True)  22.4 us
    unnamed x69, local copies, waits for them, and re-layouts  18.8 us
    all_to_all x2, blocking collectives, pair_scatter_sum(): pieces = lax.all_to_all(value, 'core', 1, 1)  16.4 us
    another operation x4, local copies, waits for them, and re-layouts, skew_table(): jnp.tile(padded[:, None, :], (1, span, 1))  11.5 us
    ppermute x4, waiting for transfers between devices, from_behind(): lax.ppermute(value, axis, [(source, source + steps) for source in range(i...  11.4 us
  transfers between devices with their start and end apart: 15, of which 11 were waited for; matrix products, arithmetic and copies ran while one was open for 21% of the time, Pallas kernels for 0%

profile of v5, /device:TPU:2, one launch (start us, length us, event | category | flops | bytes accessed | tf_op | source)
XLA Modules:
  0.0 411.6 jit_solution(6625039738910039495)
XLA Ops:
  19.8 3.9 tile.17
  29.1 3.9 tile.15
  46.8 53.9 %collective-permute-done = bf16[2048,3,256]{0,2,1:T(8,128)(2,1)} collective-permute-done((bf16[2048,3,256]{0,2,1:T(8,128)(2,1)S(1)}, bf16[2048,3,256]{0,2,1:T(8,128)(2,1)}, u32[]{:S(2)}, u32[]{:S(2)}) %collective-permute-start) | collective-permute-done | bytes 3145760 | tf_op jit(solution)/shard_map/ppermute | solution.py:21
  100.7 4.1 constant_dynamic-update-slice_fusion.4
  104.8 7.5 %convolution_convert_fusion.3 = bf16[512,768]{1,0:T(8,128)(2,1)S(1)} fusion(bf16[512,4096]{1,0:T(8,128)(2,1)} %all-gather.4.cloned.1.call-done, bf16[4096,768]{0,1:T(8,128)(2,1)} %bitcast.1), kind=kOutput, calls=%fused_computation.32 | convolution fusion | flops 3221618688 | bytes 11272192 | tf_op jit(solution)/shard_map/dot_general | solution.py:131
  112.5 3.8 collective-permute-start.1
  116.3 8.3 %collective-permute-done.3 = bf16[256,2048]{1,0:T(8,128)(2,1)} collective-permute-done((bf16[256,2048]{1,0:T(8,128)(2,1)}, bf16[256,2048]{1,0:T(8,128)(2,1)}, u32[]{:S(2)}, u32[]{:S(2)}) %collective-permute-start.3) | collective-permute-done | bytes 1048608 | tf_op jit(solution)/shard_map/ppermute | solution.py:21
  128.9 22.4 %all-gather.6.cloned.1.call-done = bf16[1,512,4096]{2,1,0:T(8,128)(2,1)} async-done(((bf16[1,32,4096]{2,1,0:T(8,128)(2,1)}), bf16[1,512,4096]{2,1,0:T(8,128)(2,1)}) %all-gather.6.cloned.1.call-update) | async-done | bytes 4194320 | tf_op jit(solution)/shard_map/all_gather | solution.py:151
  151.4 5.0 %multiply_convert_fusion = (bf16[512,256]{0,1:T(8,128)(2,1)}, f32[512,256]{0,1:T(8,128)}) fusion(f32[512,3,256]{0,2,1:T(8,128)S(1)} %multiply_add_fusion, bf16[256,4096]{1,0:T(8,128)(2,1)} %constant_dynamic-update-slice_fusion.2, bf16[1,512,4096]{2,1,0:T(8,128)(2,1)} %all-gather.6.cloned.1.call-done), kind=kOutput, calls=%fused_computation.64 | convolution fusion | flops 1074003968 | bytes 7602176 | tf_op jit(solution)/shard_map/dot_general | solution.py:152
  161.3 3.9 collective-permute-done.4
  197.2 7.3 %collective-permute-done.5 = f32[2,3,256]{0,2,1:T(8,128)S(1)} collective-permute-done((f32[2,3,256]{0,2,1:T(8,128)S(1)}, f32[2,3,256]{0,2,1:T(8,128)S(1)}, u32[]{:S(2)}, u32[]{:S(2)}) %collective-permute-start.5) | collective-permute-done | bytes 6176 | tf_op jit(solution)/shard_map/ppermute | solution.py:13
  209.0 5.3 %convolution_convert_fusion = bf16[4096,768]{0,1:T(8,128)(2,1)} fusion(bf16[512,768]{0,1:T(8,128)(2,1)S(1)} %bitcast.168, bf16[512,4096]{1,0:T(8,128)(2,1)S(1)} %copy-done.27), kind=kOutput, calls=%fused_computation.2 | convolution fusion | flops 3224371200 | bytes 11272192 | tf_op jit(solution)/shard_map/dot_general | solution.py:183
  214.3 7.1 %pad_maximum_fusion = bf16[4096,1024]{0,1:T(8,128)(2,1)} fusion(bf16[4096,256]{0,1:T(8,128)(2,1)S(1)} %copy-done.12, bf16[4096,768]{0,1:T(8,128)(2,1)} %convolution_convert_fusion), kind=kLoop, calls=%fused_computation | loop fusion | flops 16777216 | bytes 16777216 | tf_op jit(solution)/shard_map/concatenate | solution.py:187
  225.7 8.2 %all_to_all.20 = bf16[8,2,32,4096]{3,2,0,1:T(8,128)(2,1)} all-to-all(bf16[8,2,32,4096]{3,2,0,1:T(8,128)(2,1)S(1)} %copy.64), channel_id=1, replica_groups=mesh['dp'=2,'context'=8,'tchip'=8,'core'=2] {'core'}, dimensions={1} | all-to-all | bytes 8388608 | tf_op jit(solution)/shard_map/all_to_all | solution.py:52
  233.9 5.0 %reduce_sum.101 = bf16[8,32,4096]{2,1,0:T(8,128)(2,1)} reduce(bf16[8,2,32,4096]{3,2,0,1:T(8,128)(2,1)} %all_to_all.20, bf16[]{:T(256)} %constant.43.clone.1), dimensions={1}, to_apply=%region_1.2 | reduce | flops 1048576 | bytes 6291458 | tf_op jit(solution)/shard_map/reduce_sum | solution.py:53
  238.9 6.6 %bitcast_convert_fusion = bf16[512,4096]{1,0:T(8,128)(2,1)S(1)} fusion(bf16[512,3,256]{0,2,1:T(8,128)(2,1)S(1)} %copy-done.18, bf16[4096,3,256]{0,2,1:T(8,128)(2,1)} %constant_dynamic-update-slice_fusion.4), kind=kOutput, calls=%fused_computation.1 | convolution fusion | flops 3223322624 | bytes 11272192 | tf_op jit(solution)/shard_map/dot_general | solution.py:195
  246.0 8.2 %all_to_all.21 = bf16[8,2,32,4096]{3,2,0,1:T(8,128)(2,1)} all-to-all(bf16[8,2,32,4096]{3,2,0,1:T(8,128)(2,1)S(1)} %copy.70), channel_id=1, replica_groups=mesh['dp'=2,'context'=8,'tchip'=8,'core'=2] {'core'}, dimensions={1} | all-to-all | bytes 8388608 | tf_op jit(solution)/shard_map/all_to_all | solution.py:52
  254.2 3.9 all-to-all-start.1
  258.1 5.1 %reduce_sum.104 = bf16[8,32,4096]{2,1,0:T(8,128)(2,1)} reduce(bf16[8,2,32,4096]{3,2,0,1:T(8,128)(2,1)} %all_to_all.21, bf16[]{:T(256)} %constant.43.clone.1), dimensions={1}, to_apply=%region_3.4 | reduce | flops 1048576 | bytes 6291458 | tf_op jit(solution)/shard_map/reduce_sum | solution.py:53
  263.2 83.9 %all-to-all-done.1 = bf16[8,32,4096]{2,1,0:T(8,128)(2,1)S(1)} async-done(((bf16[8,32,4096]{2,1,0:T(8,128)(2,1)}), bf16[8,32,4096]{2,1,0:T(8,128)(2,1)S(1)}, u32[]{:S(2)}, u32[]{:S(2)}) %all-to-all-start.1) | async-done | bytes 2097184 | tf_op jit(solution)/shard_map/all_to_all | solution.py:54
  348.5 4.6 %all-to-all-start.3 = ((bf16[8,32,4096]{2,1,0:T(8,128)(2,1)}), bf16[8,32,4096]{2,1,0:T(8,128)(2,1)}, u32[]{:S(2)}, u32[]{:S(2)}) async-start(bf16[8,32,4096]{2,1,0:T(8,128)(2,1)} %reduce_sum.104), calls=%async_computation.3 | async-start | bytes 4194304 | tf_op jit(solution)/shard_map/all_to_all | solution.py:54
  364.5 14.0 %collective-permute-done.6 = f32[4352]{0:T(1024)S(1)} collective-permute-done((f32[4352]{0:T(1024)S(1)}, f32[4352]{0:T(1024)S(1)}, u32[]{:S(2)}, u32[]{:S(2)}) %collective-permute-start.6) | collective-permute-done | bytes 17440 | tf_op jit(solution)/shard_map/ppermute | solution.py:41
  382.3 4.7 %collective-permute-done.8 = f32[4352]{0:T(1024)S(1)} collective-permute-done((f32[4352]{0:T(1024)S(1)}, f32[4352]{0:T(1024)S(1)}, u32[]{:S(2)}, u32[]{:S(2)}) %collective-permute-start.8) | collective-permute-done | bytes 17440 | tf_op jit(solution)/shard_map/ppermute | solution.py:41
  387.1 7.8 %collective-permute-done.9 = f32[4352]{0:T(1024)S(1)} collective-permute-done((f32[4352]{0:T(1024)S(1)}, f32[4352]{0:T(1024)S(1)}, u32[]{:S(2)}, u32[]{:S(2)}) %collective-permute-start.9) | collective-permute-done | bytes 17440 | tf_op jit(solution)/shard_map/ppermute | solution.py:41
  (178 shorter events, 108.9 us)
Async XLA Ops:
  7.2 97.6 %all-gather.4.cloned.1.call-start = ((), (), s32[]{:S(2)}) async-start(), calls=%async_computation.5 | async-start | bytes 4456448 | tf_op jit(solution)/shard_map/all_gather | solution.py:126
  11.3 140.1 %all-gather.6.cloned.1.call-start = ((), (), s32[]{:S(2)}) async-start(), calls=%async_computation.7 | async-start | bytes 4456448 | tf_op jit(solution)/shard_map/all_gather | solution.py:151
  12.0 5.7 %copy-start.23 = (f32[3,3,256]{2,1,0:T(4,128)S(1)}, f32[3,3,256]{2,1,0:T(4,128)}, u32[]{:S(2)}) copy-start(f32[3,3,256]{2,1,0:T(4,128)} %param.9) | copy-start | bytes 27652
  12.0 5.8 %copy-start.21 = (f32[128,16]{0,1:T(8,128)S(1)}, f32[128,16]{0,1:T(8,128)}, u32[]{:S(2)}) copy-start(f32[128,16]{0,1:T(8,128)} %param.10) | copy-start | bytes 24580
  12.0 389.5 %reduce-scatter.2.cloned.1.call-start = ((), (), s32[]{:S(2)}) async-start(), calls=%async_computation.6 | async-start | bytes 8912896 | tf_op jit(solution)/shard_map/reduce_scatter | solution.py:190
  15.3 85.4 %collective-permute-start = (bf16[2048,3,256]{0,2,1:T(8,128)(2,1)S(1)}, bf16[2048,3,256]{0,2,1:T(8,128)(2,1)}, u32[]{:S(2)}, u32[]{:S(2)}) collective-permute-start(bf16[2048,3,256]{0,2,1:T(8,128)(2,1)S(1)} %copy.57), channel_id=1, source_target_pairs={{0,128},{128,0},{1,129},{129,1},{2,130},{130,2},{3,131},{131,3},{4... | collective-permute-start | bytes 9437192 | tf_op jit(solution)/shard_map/ppermute | solution.py:21
  17.6 107.0 %collective-permute-start.3 = (bf16[256,2048]{1,0:T(8,128)(2,1)}, bf16[256,2048]{1,0:T(8,128)(2,1)}, u32[]{:S(2)}, u32[]{:S(2)}) collective-permute-start(bf16[256,2048]{1,0:T(8,128)(2,1)} %param.8), channel_id=1, source_target_pairs={{0,128},{128,0},{1,129},{129,1},{2,130},{130,2},{3,131},{131,3},{4... | collective-permute-start | bytes 3145736 | tf_op jit(solution)/shard_map/ppermute | solution.py:21
  112.3 14.9 %copy-start.8 = (bf16[512,768]{1,0:T(8,128)(2,1)}, bf16[512,768]{1,0:T(8,128)(2,1)S(1)}, u32[]{:S(2)}) copy-start(bf16[512,768]{1,0:T(8,128)(2,1)S(1)} %convolution_convert_fusion.3) | copy-start | bytes 2359300
  112.5 14.7 %collective-permute-start.1 = (bf16[2,3,256]{0,2,1:T(8,128)(2,1)S(1)}, bf16[2,3,256]{0,2,1:T(8,128)(2,1)S(1)}, u32[]{:S(2)}, u32[]{:S(2)}) collective-permute-start(bf16[2,3,256]{0,2,1:T(8,128)(2,1)S(1)} %bitcast.169), channel_id=1, source_target_pairs={{0,16},{16,32},{32,48},{48,64},{64,80},{80,96},{96,112},{1,17},{17... | collective-permute-start | bytes 9224 | tf_op jit(solution)/shard_map/ppermute | solution.py:13
  128.9 27.4 %copy-start.4 = (f32[512,3,256]{0,2,1:T(8,128)}, f32[512,3,256]{0,2,1:T(8,128)S(1)}, u32[]{:S(2)}) copy-start(f32[512,3,256]{0,2,1:T(8,128)S(1)} %multiply_add_fusion) | copy-start | bytes 4718596
  158.9 12.4 %copy-start.6 = (bf16[16,128,256]{2,1,0:T(8,128)(2,1)S(1)}, bf16[16,128,256]{2,1,0:T(8,128)(2,1)}, u32[]{:S(2)}) copy-start(bf16[16,128,256]{2,1,0:T(8,128)(2,1)} %get-tuple-element.32) | copy-start | bytes 3145732
  158.9 6.3 %collective-permute-start.4 = (bf16[127,256]{0,1:T(8,128)(2,1)S(1)}, bf16[127,256]{0,1:T(8,128)(2,1)S(1)}, u32[]{:S(2)}, u32[]{:S(2)}) collective-permute-start(bf16[127,256]{0,1:T(8,128)(2,1)S(1)} %slice.156), channel_id=1, source_target_pairs={{16,0},{32,16},{48,32},{64,48},{80,64},{96,80},{112,96},{17,1},{33... | collective-permute-start | bytes 195080 | tf_op jit(solution)/shard_map/ppermute | solution.py:13
  173.1 5.3 %copy-start.1 = (f32[2,8,128,256]{3,2,1,0:T(8,128)S(1)}, f32[2,8,128,256]{3,2,1,0:T(8,128)}, u32[]{:S(2)}) copy-start(f32[2,8,128,256]{3,2,1,0:T(8,128)} %copy.87) | copy-start | bytes 6291460
  174.8 5.5 %copy-start.10 = (bf16[512,1,256]{0,2,1:T(8,128)(2,1)}, bf16[512,1,256]{0,2,1:T(8,128)(2,1)S(1)}, u32[]{:S(2)}) copy-start(bf16[512,1,256]{0,2,1:T(8,128)(2,1)S(1)} %get-tuple-element.39) | copy-start | bytes 786436
  174.9 5.4 %collective-permute-start.2 = (bf16[127,256]{0,1:T(8,128)(2,1)S(1)}, bf16[127,256]{0,1:T(8,128)(2,1)S(1)}, u32[]{:S(2)}, u32[]{:S(2)}) collective-permute-start(bf16[127,256]{0,1:T(8,128)(2,1)S(1)} %slice_bitcast_fusion.2), channel_id=1, source_target_pairs={{0,16},{16,32},{32,48},{48,64},{64,80},{80,96},{96,112},{1,17},{17... | collective-permute-start | bytes 195080 | tf_op jit(solution)/shard_map/ppermute | solution.py:13
  191.6 5.6 %copy-start.13 = (bf16[512,256]{0,1:T(8,128)(2,1)}, bf16[512,256]{0,1:T(8,128)(2,1)S(1)}, u32[]{:S(2)}) copy-start(bf16[512,256]{0,1:T(8,128)(2,1)S(1)} %get-tuple-element.41) | copy-start | bytes 786436
  192.9 11.5 %collective-permute-start.5 = (f32[2,3,256]{0,2,1:T(8,128)S(1)}, f32[2,3,256]{0,2,1:T(8,128)S(1)}, u32[]{:S(2)}, u32[]{:S(2)}) collective-permute-start(f32[2,3,256]{0,2,1:T(8,128)S(1)} %slice.159), channel_id=1, source_target_pairs={{16,0},{32,16},{48,32},{64,48},{80,64},{96,80},{112,96},{17,1},{33... | collective-permute-start | bytes 18440 | tf_op jit(solution)/shard_map/ppermute | solution.py:13
  209.0 5.3 %copy-start.12 = (bf16[4096,256]{0,1:T(8,128)(2,1)S(1)}, bf16[4096,256]{0,1:T(8,128)(2,1)}, u32[]{:S(2)}) copy-start(bf16[4096,256]{0,1:T(8,128)(2,1)} %fusion) | copy-start | bytes 6291460
  254.2 92.9 %all-to-all-start.1 = ((bf16[8,32,4096]{2,1,0:T(8,128)(2,1)}), bf16[8,32,4096]{2,1,0:T(8,128)(2,1)S(1)}, u32[]{:S(2)}, u32[]{:S(2)}) async-start(bf16[8,32,4096]{2,1,0:T(8,128)(2,1)} %reduce_sum.101), calls=%async_computation.1 | async-start | bytes 4194304 | tf_op jit(solution)/shard_map/all_to_all | solution.py:54
  348.5 49.8 %all-to-all-start.3 = ((bf16[8,32,4096]{2,1,0:T(8,128)(2,1)}), bf16[8,32,4096]{2,1,0:T(8,128)(2,1)}, u32[]{:S(2)}, u32[]{:S(2)}) async-start(bf16[8,32,4096]{2,1,0:T(8,128)(2,1)} %reduce_sum.104), calls=%async_computation.3 | async-start | bytes 4194304 | tf_op jit(solution)/shard_map/all_to_all | solution.py:54
  362.9 15.6 %collective-permute-start.6 = (f32[4352]{0:T(1024)S(1)}, f32[4352]{0:T(1024)S(1)}, u32[]{:S(2)}, u32[]{:S(2)}) collective-permute-start(f32[4352]{0:T(1024)S(1)} %constant_dynamic-update-slice_fusion.1), channel_id=1, source_target_pairs={{0,128},{128,0},{1,129},{129,1},{2,130},{130,2},{3,131},{131,3},{4... | collective-permute-start | bytes 52232 | tf_op jit(solution)/shard_map/ppermute | solution.py:41
  378.5 3.8 collective-permute-start.7
  382.3 4.7 %collective-permute-start.8 = (f32[4352]{0:T(1024)S(1)}, f32[4352]{0:T(1024)S(1)}, u32[]{:S(2)}, u32[]{:S(2)}) collective-permute-start(f32[4352]{0:T(1024)S(1)} %add.103), channel_id=1, source_target_pairs={{0,32},{16,48},{32,0},{48,16},{64,96},{80,112},{96,64},{112,80},{1... | collective-permute-start | bytes 52232 | tf_op jit(solution)/shard_map/ppermute | solution.py:41
  387.0 7.9 %collective-permute-start.9 = (f32[4352]{0:T(1024)S(1)}, f32[4352]{0:T(1024)S(1)}, u32[]{:S(2)}, u32[]{:S(2)}) collective-permute-start(f32[4352]{0:T(1024)S(1)} %add.104), channel_id=1, source_target_pairs={{0,64},{16,80},{32,96},{48,112},{64,0},{80,16},{96,32},{112,48},{1... | collective-permute-start | bytes 52232 | tf_op jit(solution)/shard_map/ppermute | solution.py:41
  (22 other events, 45.9 us)
Sparse Core Ops, SparseCore 0:
  11.4 76.3 all-gather.3
  90.6 60.7 all-gather.5
  221.6 100.5 reduce-scatter.1
